TPU v7x, 32 devices: a whole 2x2x4 slice. The times are simulated.
32 devices in a mesh: ref: 4 (over x, core), dom: 8 (over z, y).
Axes of the slice: x: 2, y: 2, z: 4, core: 2. Of those that a mesh axis runs over, the one named last changes fastest.
Arguments:
- particles: bfloat16 [512, 7168], P(('ref', 'dom')), may hold values from -16 to 16
- offsets: int32 [512], P(('ref', 'dom')), may hold values from 0 to 8, as said below
- references: bfloat16 [512, 7168], P('ref'), may hold values from -0.6 to 0.6
- noise_weight: float32 [3584], replicated, may hold values from 0.06 to 0.24
- ref_class: int32 [512], replicated, may hold values from 0 to 7
- ref_orient: int32 [512], replicated, may hold values from 0 to 63
- class_logprior: float32 [8], replicated, may hold values from -1 to 1
- orient_logprior: float32 [64], replicated, may hold values from -1 to 1
Outputs:
- log_post: float32 [512, 9, 512], P(('ref', 'dom'))
- class_sums: float32 [8, 7168], P(None, ('ref', 'dom'))
Inputs may be any that keep to these rules, and one draw needn't show every extreme that they name: `offsets`: index of the prior's centre: horizontal step (o mod 3) - 1 pixels, vertical step floor(o / 3) - 1 pixels.
All inputs are finite; a program needn't handle non-finite values.
Results may differ from a plain program's by a relative error of at most 0.0042.
Values may be sent and summed in bfloat16 or wider, within the bound.
No kernel may reach another device: no remote copies, remote signals or barrier semaphores. Data moves between devices by JAX's collectives and lax.ppermute only.
A program may use at most 64 MiB of HBM per device.

v0:
```python
import math

import jax
import jax.numpy as jnp
from jax import lax
from jax.sharding import PartitionSpec as P

SHIFTS = 9


def shift_tables(count):
    coeffs = jnp.arange(count, dtype=jnp.int32)
    column_freq = (coeffs % 56).astype(jnp.float32)
    row_freq = (coeffs // 56 - 32).astype(jnp.float32)
    shift_ids = jnp.arange(SHIFTS, dtype=jnp.int32)
    step_right = (shift_ids % 3 - 1).astype(jnp.float32)
    step_down = (shift_ids // 3 - 1).astype(jnp.float32)
    turning = (
        2.0
        * math.pi
        / 96.0
        * (step_right[:, None] * column_freq[None, :] + step_down[:, None] * row_freq[None, :])
    )
    return (jnp.cos(turning), jnp.sin(turning))


def centre_prior(offsets):
    shift_ids = jnp.arange(SHIFTS, dtype=jnp.int32)
    step_right = (shift_ids % 3 - 1).astype(jnp.float32)
    step_down = (shift_ids // 3 - 1).astype(jnp.float32)
    centre_right = (offsets % 3 - 1).astype(jnp.float32)
    centre_down = (offsets // 3 - 1).astype(jnp.float32)
    apart_right = step_right[None, :] - centre_right[:, None]
    apart_down = step_down[None, :] - centre_down[:, None]
    return -0.5 * (apart_right * apart_right + apart_down * apart_down)


def aligned_stack(real_part, imag_part, cosine_table, sine_table, twice):
    turned_real = (
        real_part[:, None, :] * cosine_table[None] - imag_part[:, None, :] * sine_table[None]
    )
    turned_imag = (
        real_part[:, None, :] * sine_table[None] + imag_part[:, None, :] * cosine_table[None]
    )
    stacked_rows = real_part.shape[0] * cosine_table.shape[0]
    scaled_real = (
        (turned_real * twice[None, None, :])
        .astype(jnp.bfloat16)
        .reshape(stacked_rows, real_part.shape[1])
    )
    scaled_imag = (
        (turned_imag * twice[None, None, :])
        .astype(jnp.bfloat16)
        .reshape(stacked_rows, real_part.shape[1])
    )
    return (scaled_real, scaled_imag)


def contract(left, right):
    return lax.dot_general(
        left, right, (((1,), (1,)), ((), ())), preferred_element_type=jnp.float32
    )


def local(
    particles,
    offsets,
    references,
    noise_weight,
    ref_class,
    ref_orient,
    class_logprior,
    orient_logprior,
):
    local_rows = particles.shape[0]
    coef_total = particles.shape[1] // 2
    ref_total = ref_class.shape[0]
    class_count = class_logprior.shape[0]
    cosine_table, sine_table = shift_tables(coef_total)
    twice = 2.0 * noise_weight
    values = particles.astype(jnp.float32)
    real_part = values[:, :coef_total]
    imag_part = values[:, coef_total:]
    scaled_real, scaled_imag = aligned_stack(real_part, imag_part, cosine_table, sine_table, twice)
    class_table = (ref_class[:, None] == jnp.arange(class_count, dtype=jnp.int32)[None, :]).astype(
        jnp.float32
    )
    orient_table = (
        ref_orient[:, None] == jnp.arange(orient_logprior.shape[0], dtype=jnp.int32)[None, :]
    ).astype(jnp.float32)
    prior = jnp.dot(class_table, class_logprior, precision=lax.Precision.HIGHEST) + jnp.dot(
        orient_table, orient_logprior, precision=lax.Precision.HIGHEST
    )
    segment = lax.all_gather(references, "ref", axis=0, tiled=True)
    cross_piece = contract(scaled_real, segment[:, :coef_total]) + contract(
        scaled_imag, segment[:, coef_total:]
    )
    wide = segment.astype(jnp.float32)
    norm_piece = jnp.sum(
        noise_weight[None, :]
        * (
            wide[:, :coef_total] * wide[:, :coef_total]
            + wide[:, coef_total:] * wide[:, coef_total:]
        ),
        axis=1,
    )
    scores = (
        cross_piece.reshape(local_rows, SHIFTS, ref_total)
        - norm_piece[None, None, :]
        + prior[None, None, :]
        + centre_prior(offsets)[:, :, None]
    )
    row_peak = jnp.max(scores, axis=(1, 2), keepdims=True)
    log_total = row_peak + jnp.log(jnp.sum(jnp.exp(scores - row_peak), axis=(1, 2), keepdims=True))
    log_post = scores - log_total
    class_post = jnp.dot(
        jnp.exp(log_post).reshape(local_rows * SHIFTS, ref_total),
        class_table,
        precision=lax.Precision.HIGHEST,
    ).reshape(local_rows, SHIFTS, class_count)
    sums_real = jnp.einsum("ntc,nk->tck", class_post, real_part, precision=lax.Precision.HIGHEST)
    sums_imag = jnp.einsum("ntc,nk->tck", class_post, imag_part, precision=lax.Precision.HIGHEST)
    class_real = jnp.einsum(
        "tk,tck->ck", cosine_table, sums_real, precision=lax.Precision.HIGHEST
    ) - jnp.einsum("tk,tck->ck", sine_table, sums_imag, precision=lax.Precision.HIGHEST)
    class_imag = jnp.einsum(
        "tk,tck->ck", sine_table, sums_real, precision=lax.Precision.HIGHEST
    ) + jnp.einsum("tk,tck->ck", cosine_table, sums_imag, precision=lax.Precision.HIGHEST)
    devices = lax.axis_size(("ref", "dom"))
    partial_value = jnp.concatenate([class_real, class_imag], axis=1) * (
        1.0 / math.sqrt(local_rows * devices)
    )
    by_ref = lax.psum_scatter(partial_value, "ref", scatter_dimension=1, tiled=True)
    class_sums = lax.psum_scatter(by_ref, "dom", scatter_dimension=1, tiled=True)
    return (log_post, class_sums)


def solution(mesh):
    return jax.shard_map(
        local,
        mesh=mesh,
        in_specs=(
            P(("ref", "dom"), None),
            P(("ref", "dom")),
            P("ref", None),
            P(),
            P(),
            P(),
            P(),
            P(),
        ),
        out_specs=(P(("ref", "dom"), None, None), P(None, ("ref", "dom"))),
        check_vma=False,
    )
```

profile of v0, /device:TPU:0, one launch (start us, length us, event | category | flops | bytes accessed | tf_op | source)
XLA Modules:
  0.0 185.6 jit_solution(1303714036700717217)
XLA Ops:
  7.2 0.0 copy-start
  7.2 0.0 all-gather.2.cloned.1.call-start
  7.2 0.7 all-gather.2.cloned.1.call-update
  7.9 0.0 reduce-scatter.5.cloned.1.call-start
  8.0 0.1 sub.250
  8.1 0.7 fusion.42
  8.7 0.1 sub.241
  8.8 0.1 sub.251
  8.9 0.1 sub.246
  9.0 0.1 sub.236
  9.1 0.1 sub.247
  9.2 1.0 fusion.45
  10.2 1.6 fusion.22
  11.8 4.0 %multiply_subtract_fusion = (f32[16,9,3584]{2,1,0:T(8,128)}, f32[16,9,3584]{2,1,0:T(8,128)}) fusion(f32[9,3584]{1,0:T(8,128)S(1)} %get-tuple-element.20, f32[16,3584]{1,0:T(8,128)S(1)} %get-tuple-element.17, f32[9,3584]{1,0:T(8,128)S(1)} %get-tuple-element.21, f32[16,3584]{1,0:T(8,128)S(1)} %get-tuple-element.16), kind=kLoop, calls=%fused_computation.12 | loop fusion | flops 3096576 | bytes 4845568 | tf_op jit(solution)/shard_map/sub | solution.py:40
  15.8 3.2 %add.206 = f32[144,3584]{1,0:T(8,128)} reshape(f32[16,9,3584]{2,1,0:T(8,128)} %get-tuple-element.15) | data formatting | bytes 4128768 | tf_op jit(solution)/shard_map/add | solution.py:43
  19.0 0.0 copy-start.6
  19.0 0.0 copy-start.7
  19.0 0.0 copy-start.8
  19.0 0.0 copy-start.5
  19.0 2.9 %sub.231 = f32[144,3584]{1,0:T(8,128)S(1)} reshape(f32[16,9,3584]{2,1,0:T(8,128)} %get-tuple-element.14) | data formatting | bytes 4128768 | tf_op jit(solution)/shard_map/sub | solution.py:40
  21.9 0.0 copy-done
  21.9 0.0 copy-done.6
  21.9 0.1 fusion.28
  22.0 0.0 copy-done.7
  22.0 0.0 copy-done.8
  22.0 0.3 fusion.12
  22.4 0.0 copy-done.5
  22.4 42.2 %all-gather.2.cloned.1.call-done = bf16[512,7168]{1,0:T(8,128)(2,1)} async-done(((bf16[128,7168]{1,0:T(8,128)(2,1)}), bf16[512,7168]{1,0:T(8,128)(2,1)}) %all-gather.2.cloned.1.call-update) | async-done | bytes 7340048 | tf_op jit(solution)/shard_map/all_gather | solution.py:94
  64.6 10.2 %convert_element_type.131 = f32[512,7168]{1,0:T(8,128)} convert(bf16[512,7168]{1,0:T(8,128)(2,1)} %all-gather.2.cloned.1.call-done) | non-fusion elementwise | flops 3670016 | bytes 22020096 | tf_op jit(solution)/shard_map/convert_element_type | solution.py:98
  74.8 0.0 copy-start.1
  74.8 6.1 %fusion.2 = f32[512]{0:T(512)S(1)} fusion(f32[512,7168]{1,0:T(8,128)} %convert_element_type.131, f32[3584]{0:T(1024)S(1)} %copy-done.5), kind=kLoop, calls=%fused_computation.3 | loop fusion | flops 9174528 | bytes 14696448 | tf_op jit(solution)/shard_map/reduce_sum | solution.py:99
  80.9 1.2 copy-done.1
  82.1 0.6 copy-done.3
  82.7 1.3 fusion.3
  84.1 0.0 copy-start.2
  84.1 1.5 fusion.15
  85.6 0.0 copy-start.4
  85.6 0.1 reduce_max.14
  85.7 0.1 reduce_max.18
  85.8 0.1 sub.253
  85.8 0.1 sub.254
  86.0 0.2 exponential_reduce_fusion
  86.2 0.1 reduce_sum.27
  86.3 0.1 reduce_sum.28
  86.4 0.1 sub.259
  86.5 0.1 sub.260
  86.6 0.1 subtract_exponential_fusion
  86.8 1.0 fusion.33
  87.8 0.1 copy.17
  88.0 0.0 copy-done.2
  88.0 0.5 convolution_bitcast_fusion
  88.5 0.0 copy-done.4
  88.5 0.7 multiply_reduce_fusion.3
  89.3 0.7 maximum_multiply_fusion
  90.0 0.0 reduce-scatter.5.cloned.1.call-update
  90.0 0.0 reduce-scatter.7.cloned.1.call-start
  90.1 0.1 add_multiply_fusion.1
  90.2 19.9 %reduce-scatter.5.cloned.1.call-done = f32[8,1792]{1,0:T(8,128)} async-done(((f32[8,7168]{1,0:T(8,128)}), f32[8,1792]{1,0:T(8,128)}) %reduce-scatter.5.cloned.1.call-update) | async-done | bytes 57360 | tf_op jit(solution)/shard_map/reduce_scatter | solution.py:133
  110.1 2.1 %copy.44 = f32[8,1792]{0,1:T(8,128)} copy(f32[8,1792]{1,0:T(8,128)} %reduce-scatter.5.cloned.1.call-done) | data formatting | bytes 114688
  112.2 0.0 reduce-scatter.7.cloned.1.call-update
  112.2 0.1 add_subtract_fusion
  112.3 0.9 copy.19
  113.2 64.2 %reduce-scatter.7.cloned.1.call-done = f32[224,8]{1,0:T(8,128)} async-done(((f32[1792,8]{1,0:T(8,128)}), f32[224,8]{1,0:T(8,128)}) %reduce-scatter.7.cloned.1.call-update) | async-done | bytes 7184
  177.5 1.6 copy.45
  (13 shorter events, 0.2 us)
Async XLA Ops:
  7.2 14.7 %copy-start = (f32[8]{0:T(128)S(1)}, f32[8]{0:T(128)}, u32[]{:S(2)}) copy-start(f32[8]{0:T(128)} %param.14) | copy-start | bytes 100
  7.2 57.4 %all-gather.2.cloned.1.call-start = ((), (), s32[]{:S(2)}) async-start(), calls=%async_computation.2 | async-start | bytes 9175040 | tf_op jit(solution)/shard_map/all_gather | solution.py:94
  7.9 102.2 %reduce-scatter.5.cloned.1.call-start = ((), (), s32[]{:S(2)}) async-start(), calls=%async_computation.3 | async-start | bytes 286720 | tf_op jit(solution)/shard_map/reduce_scatter | solution.py:133
  19.0 2.9 %copy-start.6 = (s32[512]{0:T(512)S(1)}, s32[512]{0:T(512)}, u32[]{:S(2)}) copy-start(s32[512]{0:T(512)} %param.12) | copy-start | bytes 6148
  19.0 3.0 %copy-start.7 = (s32[512]{0:T(512)S(1)}, s32[512]{0:T(512)}, u32[]{:S(2)}) copy-start(s32[512]{0:T(512)} %param.13) | copy-start | bytes 6148
  19.0 3.0 %copy-start.8 = (f32[64]{0:T(128)S(1)}, f32[64]{0:T(128)}, u32[]{:S(2)}) copy-start(f32[64]{0:T(128)} %param.15) | copy-start | bytes 772
  19.0 3.4 %copy-start.5 = (f32[3584]{0:T(1024)S(1)}, f32[3584]{0:T(1024)}, u32[]{:S(2)}) copy-start(f32[3584]{0:T(1024)} %param.11) | copy-start | bytes 43012
  74.8 7.3 %copy-start.1 = (bf16[512,7168]{1,0:T(8,128)(2,1)S(1)}, bf16[512,7168]{1,0:T(8,128)(2,1)}, u32[]{:S(2)}) copy-start(bf16[512,7168]{1,0:T(8,128)(2,1)} %all-gather.2.cloned.1.call-done) | copy-start | bytes 22020100
  74.8 7.9 %copy-start.3 = (f32[144,3584]{1,0:T(8,128)S(1)}, f32[144,3584]{1,0:T(8,128)}, u32[]{:S(2)}) copy-start(f32[144,3584]{1,0:T(8,128)} %add.206) | copy-start | bytes 6193156
  84.1 3.9 %copy-start.2 = (bf16[16,7168]{1,0:T(8,128)(2,1)S(1)}, bf16[16,7168]{1,0:T(8,128)(2,1)}, u32[]{:S(2)}) copy-start(bf16[16,7168]{1,0:T(8,128)(2,1)} %param.8) | copy-start | bytes 688132
  85.6 2.9 %copy-start.4 = (f32[3584,9]{0,1:T(8,128)S(1)}, f32[3584,9]{0,1:T(8,128)}, u32[]{:S(2)}) copy-start(f32[3584,9]{0,1:T(8,128)} %get-tuple-element.19) | copy-start | bytes 387076
  90.0 87.4 %reduce-scatter.7.cloned.1.call-start = ((), (), s32[]{:S(2)}) async-start(), calls=%async_computation.4 | async-start | bytes 1032192
Sparse Core Ops, SparseCore 0:
  9.5 55.0 all-gather.1
  90.2 19.8 reduce-scatter.4
  113.4 63.9 reduce-scatter.6
where the time goes:
time: 186 us
  waiting for transfers between devices  127 us (68%)
  other arithmetic  24.2 us (13%)
  local copies, waits for them, and re-layouts  14.7 us (8%)
  between operations  14 us (8%)
  matrix products  5.57 us (3%)
    unnamed x4, waiting for transfers between devices  64.9 us
    all_gather x1, waiting for transfers between devices, local(): segment = lax.all_gather(references, 'ref', axis=0, tiled=True)  42.2 us
    reduce_scatter x1, waiting for transfers between devices, local(): lax.psum_scatter(partial_value, 'ref', scatter_dimension=1, tiled=True)  19.9 us
    convert_element_type x1, other arithmetic, local(): wide = segment.astype(jnp.float32)  10.2 us
    unnamed x21, local copies, waits for them, and re-layouts  6.36 us
    reduce_sum x1, other arithmetic, local(): jnp.sum(noise_weight[None, :] * (wide[:, :coef_total] * wide[:, :coef_tot...  6.08 us
    sub x1, other arithmetic, aligned_stack(): real_part[:, None, :] * cosine_table[None]  4 us
  transfers between devices with their start and end apart: 3, of which 3 were waited for; matrix products, arithmetic and copies ran while one was open for 8% of the time, Pallas kernels for 0%

commit v1 on v0

v1 whole, which is shorter than its diff:
```python
import functools
import math

import jax
import jax.numpy as jnp
import numpy as np
from jax import lax
from jax.experimental import pallas as pl
from jax.experimental.pallas import tpu as pltpu
from jax.sharding import PartitionSpec as P

SHIFTS = 9
PAIRS = 4
LANES = 128
CHUNK = 512
VMEM_LIMIT = 24 * 1024 * 1024


def turning_table(count):
    coeffs = np.arange(count)
    column_freq = (coeffs % 56).astype(np.float32)
    row_freq = (coeffs // 56 - 32).astype(np.float32)
    shift_ids = np.arange(SHIFTS - PAIRS, SHIFTS)
    right = (shift_ids % 3 - 1).astype(np.float32)
    down = (shift_ids // 3 - 1).astype(np.float32)
    turning = np.float32(2.0 * math.pi / 96.0) * (
        right[:, None] * column_freq[None, :] + down[:, None] * row_freq[None, :]
    )
    return np.concatenate([np.cos(turning), np.sin(turning)], axis=0).astype(np.float32)


def three_parts(value):
    high = value.astype(jnp.bfloat16)
    rest = value - high.astype(jnp.float32)
    middle = rest.astype(jnp.bfloat16)
    low = (rest - middle.astype(jnp.float32)).astype(jnp.bfloat16)
    return high, middle, low


def chunks(total):
    size = CHUNK if total % CHUNK == 0 else LANES
    return [(start, size) for start in range(0, total, size)]


def dot_nt(left, right):
    return lax.dot_general(
        left, right, (((1,), (1,)), ((), ())), preferred_element_type=jnp.float32
    )


def score_body(first, classes, own_ref, peer_ref, part_ref, table_ref, weight_ref, bias_ref,
               class_ref, tag_ref, scores_ref, stats_ref, bias_out_ref=None):
    rows, width = part_ref.shape
    coefs = width // 2
    block = own_ref.shape[0]
    cross = jnp.zeros((SHIFTS * rows, 2 * block), jnp.float32)
    norm = jnp.zeros((2 * block, LANES), jnp.float32)
    for start, size in chunks(coefs):
        re = pl.ds(start, size)
        im = pl.ds(coefs + start, size)
        weight = weight_ref[:, re]
        twice = 2.0 * weight
        table = table_ref[:, re] * twice
        x = part_ref[:, re].astype(jnp.float32)
        y = part_ref[:, im].astype(jnp.float32)
        real = [None] * SHIFTS
        imag = [None] * SHIFTS
        middle = SHIFTS // 2
        real[middle] = (x * twice).astype(jnp.bfloat16)
        imag[middle] = (y * twice).astype(jnp.bfloat16)
        for p in range(PAIRS):
            cosine = table[p : p + 1]
            sine = table[PAIRS + p : PAIRS + p + 1]
            xc, ys, xs, yc = x * cosine, y * sine, x * sine, y * cosine
            t = middle + 1 + p
            real[t] = (xc - ys).astype(jnp.bfloat16)
            imag[t] = (xs + yc).astype(jnp.bfloat16)
            real[SHIFTS - 1 - t] = (xc + ys).astype(jnp.bfloat16)
            imag[SHIFTS - 1 - t] = (yc - xs).astype(jnp.bfloat16)
        refs_re = jnp.concatenate([own_ref[:, re], peer_ref[:, re]], axis=0)
        refs_im = jnp.concatenate([own_ref[:, im], peer_ref[:, im]], axis=0)
        cross += dot_nt(jnp.concatenate(real, axis=0), refs_re)
        cross += dot_nt(jnp.concatenate(imag, axis=0), refs_im)
        if first:
            for lane in range(0, size, LANES):
                a = refs_re[:, lane : lane + LANES].astype(jnp.float32)
                b = refs_im[:, lane : lane + LANES].astype(jnp.float32)
                norm += weight[:, lane : lane + LANES] * (a * a + b * b)
    bias = bias_ref[...]
    if first:
        bias = bias - jnp.sum(jnp.transpose(norm), axis=0, keepdims=True)
        bias_out_ref[...] = bias
    scores = cross + bias
    scores_ref[...] = scores.reshape(SHIFTS, rows, 2 * block)
    peak = scores[:rows]
    for t in range(1, SHIFTS):
        peak = jnp.maximum(peak, scores[t * rows : (t + 1) * rows])
    peak = jnp.max(peak, axis=1, keepdims=True)
    mass = jnp.exp(scores - jnp.concatenate([peak] * SHIFTS, axis=0))
    lanes = lax.broadcasted_iota(jnp.int32, (2 * block, LANES), 1)
    table = (lanes == class_ref[...]).astype(jnp.float32).astype(jnp.bfloat16)
    high, mid, low = three_parts(mass)
    by_class = jnp.dot(jnp.concatenate([high, mid, low], axis=0), table,
                       preferred_element_type=jnp.float32)
    span = SHIFTS * rows
    by_class = by_class[:span] + by_class[span : 2 * span] + by_class[2 * span :]
    stats = by_class[:rows]
    for t in range(1, SHIFTS):
        stats += pltpu.roll(by_class[t * rows : (t + 1) * rows], classes * t, 1)
    lane = lax.broadcasted_iota(jnp.int32, (rows, LANES), 1)
    stats = jnp.where(lane == SHIFTS * classes, peak, stats)
    stats = jnp.where(lane == SHIFTS * classes + 1, tag_ref[...], stats)
    stats_ref[...] = stats


def score(first, classes, own, peer, part, table, weight, bias, class_col, tag):
    rows, width = part.shape
    block = own.shape[0]
    outs = [
        jax.ShapeDtypeStruct((SHIFTS, rows, 2 * block), jnp.float32),
        jax.ShapeDtypeStruct((rows, LANES), jnp.float32),
    ]
    if first:
        outs.append(jax.ShapeDtypeStruct((1, 2 * block), jnp.float32))
    flops = 2 * SHIFTS * rows * width * 2 * block
    return pl.pallas_call(
        functools.partial(score_body, first, classes),
        out_shape=outs,
        name="score_own" if first else "score_other",
        compiler_params=pltpu.CompilerParams(vmem_limit_bytes=VMEM_LIMIT),
        cost_estimate=pl.CostEstimate(
            flops=flops, bytes_accessed=2 * (2 * block + rows) * width, transcendentals=0
        ),
    )(own, peer, part, table, weight, bias, class_col, tag)


def sums_body(groups, classes, scale, place_ref, table_ref, *refs):
    stats = refs[:groups]
    parts = refs[groups : 2 * groups]
    keep_ref, send_ref, total_ref = refs[2 * groups :]
    rows = parts[0].shape[0]
    width = parts[0].shape[1]
    coefs = width // 2
    span = width // groups
    used = SHIFTS * classes
    chip, core, dom = place_ref[0], place_ref[1], place_ref[2]
    lane = lax.broadcasted_iota(jnp.int32, (rows, LANES), 1)
    shift = lane // classes
    right = (shift % 3 - 1).astype(jnp.float32)
    down = (shift // 3 - 1).astype(jnp.float32)
    posts = []
    for slot in range(groups):
        seen = [stats[i][(slot ^ i) * rows : ((slot ^ i) + 1) * rows] for i in range(groups)]
        peaks = [value[:, used : used + 1] for value in seen]
        peak = functools.reduce(jnp.maximum, peaks)
        mass = sum(value * jnp.exp(low - peak) for value, low in zip(seen, peaks))
        centre = stats[slot][:rows, used + 1 : used + 2].astype(jnp.int32)
        across = right - (centre % 3 - 1).astype(jnp.float32)
        along = down - (centre // 3 - 1).astype(jnp.float32)
        prior = -0.5 * (across * across + along * along)
        mass = jnp.where(lane < used, mass * jnp.exp(prior), 0.0)
        whole = jnp.sum(mass, axis=1, keepdims=True)
        posts.append(mass / whole)
        if slot == 0:
            total_ref[...] = prior - (peak + jnp.log(whole))
    post = jnp.transpose(jnp.concatenate(posts, axis=0))
    middle = SHIFTS // 2
    by_shift = [post[t * classes : (t + 1) * classes] for t in range(SHIFTS)]
    even = [by_shift[middle]]
    odd = []
    for p in range(PAIRS):
        t = middle + 1 + p
        even.append(by_shift[t] + by_shift[SHIFTS - 1 - t])
        odd.append(by_shift[t] - by_shift[SHIFTS - 1 - t])
    even = jnp.concatenate(three_parts(jnp.concatenate(even, axis=0)), axis=0)
    odd = jnp.concatenate(three_parts(jnp.concatenate(odd, axis=0)), axis=0)
    sign = jnp.where(chip < groups // 2, -1.0, 1.0)
    column = chip * span
    other = lax.rem(column + coefs, width)
    base = lax.rem(column, coefs)
    step = CHUNK if span % CHUNK == 0 else LANES
    pieces = []
    for start in range(0, span, step):
        u = jnp.concatenate(
            [part[:, pl.ds(pl.multiple_of(column + start, LANES), step)] for part in parts], axis=0
        )
        v = jnp.concatenate(
            [part[:, pl.ds(pl.multiple_of(other + start, LANES), step)] for part in parts], axis=0
        )
        table = table_ref[:, pl.ds(pl.multiple_of(base + start, LANES), step)]
        evens = jnp.dot(even, u, preferred_element_type=jnp.float32)
        odds = jnp.dot(odd, v, preferred_element_type=jnp.float32)
        ne = (PAIRS + 1) * classes
        no = PAIRS * classes
        evens = evens[:ne] + (evens[ne : 2 * ne] + evens[2 * ne :])
        odds = odds[:no] + (odds[no : 2 * no] + odds[2 * no :])
        direct = evens[:classes]
        turned = jnp.zeros_like(direct)
        for p in range(PAIRS):
            direct += table[p : p + 1] * evens[(p + 1) * classes : (p + 2) * classes]
            turned += table[PAIRS + p : PAIRS + p + 1] * odds[p * classes : (p + 1) * classes]
        pieces.append((direct + sign * turned) * scale)
    result = jnp.concatenate(pieces, axis=1)
    slots = keep_ref.shape[0]
    part_width = keep_ref.shape[2]
    for half in range(2):
        for d in range(slots):
            at = (half * slots + d) * part_width
            piece = result[:, at : at + part_width]

            @pl.when(core == half)
            def _(piece=piece, d=d):
                keep_ref[lax.bitwise_xor(dom, d)] = piece

            @pl.when(core != half)
            def _(piece=piece, d=d):
                send_ref[lax.bitwise_xor(dom, d)] = piece


def partial_sums(groups, classes, scale, slots, columns, place, table, stats, parts):
    rows = parts[0].shape[0]
    piece = jax.ShapeDtypeStruct((slots, classes, columns), jnp.float32)
    vmem = pl.BlockSpec(memory_space=pltpu.VMEM)
    return pl.pallas_call(
        functools.partial(sums_body, groups, classes, scale),
        out_shape=[piece, piece, jax.ShapeDtypeStruct((rows, LANES), jnp.float32)],
        in_specs=[pl.BlockSpec(memory_space=pltpu.SMEM)] + [vmem] * (1 + 2 * groups),
        out_specs=[vmem] * 3,
        name="class_partial",
        compiler_params=pltpu.CompilerParams(vmem_limit_bytes=VMEM_LIMIT),
        cost_estimate=pl.CostEstimate(flops=1000000, bytes_accessed=1000000, transcendentals=0),
    )(place, table, *stats, *parts)


def local(refs_axis, dom_axis, particles, offsets, references, noise_weight, ref_class, ref_orient,
          class_logprior, orient_logprior):
    rows, width = particles.shape
    coefs = width // 2
    block = references.shape[0]
    classes = class_logprior.shape[0]
    groups = refs_axis // 2
    me = lax.axis_index("ref")
    dom = lax.axis_index("dom")

    def swap(value, axis, size, bit):
        return lax.ppermute(value, axis, [(i, i ^ bit) for i in range(size)])

    others = [swap(particles, "ref", refs_axis, 2 * i) for i in range(1, groups)]
    peer_refs = swap(references, "ref", refs_axis, 1)

    table = jnp.asarray(turning_table(coefs))
    weight = noise_weight[None, :]
    class_row = jnp.sum(
        jnp.where(jnp.arange(classes)[:, None] == ref_class[None, :], class_logprior[:, None], 0.0),
        axis=0,
    )
    orient_row = jnp.sum(
        jnp.where(
            jnp.arange(orient_logprior.shape[0])[:, None] == ref_orient[None, :],
            orient_logprior[:, None],
            0.0,
        ),
        axis=0,
    )
    prior = class_row + orient_row

    def mine(row):
        return jnp.concatenate(
            [lax.dynamic_slice(row, ((me ^ i) * block,), (block,)) for i in range(2)]
        )

    bias = mine(prior)[None, :]
    class_col = mine(ref_class)[:, None]
    tag = offsets.astype(jnp.float32)[:, None]
    fixed = (references, peer_refs)
    own_scores, own_stats, bias = score(
        True, classes, *fixed, particles, table, weight, bias, class_col, tag
    )
    sent_scores, stats = [], [own_stats]
    for other in others:
        value, stat = score(False, classes, *fixed, other, table, weight, bias, class_col, tag)
        sent_scores.append(value)
        stats.append(stat)
    stats = jnp.concatenate(stats, axis=0)
    seen = [stats] + [swap(stats, "ref", refs_axis, 2 * i) for i in range(1, groups)]
    place = jnp.stack([me // 2, me % 2, dom]).astype(jnp.int32)
    scale = 1.0 / math.sqrt(rows * refs_axis * dom_axis)
    columns = width // (refs_axis * dom_axis)
    keep, send, total = partial_sums(
        groups, classes, scale, dom_axis, columns, place, table, seen, [particles] + others
    )
    keep = keep + swap(send, "ref", refs_axis, 1)
    slots = dom_axis
    while slots > 1:
        slots //= 2
        keep = keep[:slots] + swap(keep[slots:], "dom", dom_axis, slots)
    class_sums = keep[0]

    got = [own_scores] + [
        swap(value, "ref", refs_axis, 2 * (i + 1)) for i, value in enumerate(sent_scores)
    ]
    blocks = []
    for value in got:
        blocks += [value[:, :, :block], value[:, :, block:]]
    bit = 1
    while bit < refs_axis:
        blocks = [
            jnp.where((me & bit) != 0, blocks[j ^ bit], blocks[j]) for j in range(refs_axis)
        ]
        bit *= 2
    lift = jnp.transpose(total[:, : SHIFTS * classes].reshape(rows, SHIFTS, classes)[:, :, 0])
    log_post = jnp.concatenate(blocks, axis=2) + lift[:, :, None]
    return (jnp.transpose(log_post, (1, 0, 2)), class_sums)


def solution(mesh):
    return jax.shard_map(
        functools.partial(local, mesh.shape["ref"], mesh.shape["dom"]),
        mesh=mesh,
        in_specs=(
            P(("ref", "dom"), None),
            P(("ref", "dom")),
            P("ref", None),
            P(),
            P(),
            P(),
            P(),
            P(),
        ),
        out_specs=(P(("ref", "dom"), None, None), P(None, ("ref", "dom"))),
        check_vma=False,
    )
```

time: 186 us -> 39.5 us (0.21)
  waiting for transfers between devices: 127 us -> 13.9 us
  other arithmetic: 24.2 us -> 3.79 us
  between operations: 14 us -> 0.75 us
  local copies, waits for them, and re-layouts: 14.7 us -> 5.32 us
  starting transfers between devices: 0.12 us -> 9.22 us
  Pallas kernels: 0 us -> 6.13 us
  matrix products: 5.57 us -> 0 us
    unnamed x4 -> x0, waiting for transfers between devices: 64.9 us -> none
    all_gather x1 -> x0, waiting for transfers between devices: 42.2 us -> none  [local(): segment = lax.all_gather(references, 'ref', axis=0, tiled=True)]
    reduce_scatter x1 -> x0, waiting for transfers between devices: 19.9 us -> none  [local(): lax.psum_scatter(partial_value, 'ref', scatter_dimension=1, tiled=True)]
    ppermute x0 -> x8, waiting for transfers between devices: none -> 13.9 us  [swap(): return lax.ppermute(value, axis, [(i, i ^ bit) for i in range(size)])]
    convert_element_type x4 -> x0, other arithmetic: 10.9 us -> none  [the longest x1 10.2 us: local(): wide = segment.astype(jnp.float32)]
    ppermute x0 -> x8, starting transfers between devices: none -> 9.22 us  [swap(): return lax.ppermute(value, axis, [(i, i ^ bit) for i in range(size)])]
    pallas_call x0 -> x3, Pallas kernels: none -> 6.13 us  [the longest x2 3.94 us: score(): pl.pallas_call(functools.partial(score_body, first, classes), out_shape=o...]
    dot_general x7 -> x0, matrix products: 5.57 us -> none  [the longest x2 2.82 us: contract(): lax.dot_general(left, right, (((1,), (1,)), ((), ())), preferred_element_...]
  transfers between devices with their start and end apart: 3 -> 8, of which waited for: 3 -> 6; matrix products, arithmetic and copies ran while one was open for 8% -> 13% of each run, Pallas kernels for 0% -> 5%
where the time goes in v1:
time: 39.5 us; the launch traced here: 39.1 us
  waiting for transfers between devices  13.9 us (35%)
  starting transfers between devices  9.22 us (23%)
  Pallas kernels  6.13 us (16%)
  local copies, waits for them, and re-layouts  5.32 us (13%)
  other arithmetic  3.79 us (10%)
  between operations  0.75 us (2%)
    ppermute x8, waiting for transfers between devices, swap(): return lax.ppermute(value, axis, [(i, i ^ bit) for i in range(size)])  13.9 us
    ppermute x8, starting transfers between devices, swap(): return lax.ppermute(value, axis, [(i, i ^ bit) for i in range(size)])  9.22 us
    pallas_call x2, Pallas kernels, score(): pl.pallas_call(functools.partial(score_body, first, classes), out_shape=o...  3.94 us
    unnamed x9, local copies, waits for them, and re-layouts  3.34 us
    pallas_call x1, Pallas kernels, partial_sums(): pl.pallas_call(functools.partial(sums_body, groups, classes, scale), out_...  2.19 us
    dynamic_slice x2, local copies, waits for them, and re-layouts, mine(): lax.dynamic_slice(row, ((me ^ i) * block,), (block,))  0.91 us
    transpose x1, other arithmetic, local(): return (jnp.transpose(log_post, (1, 0, 2)), class_sums)  0.81 us
    reduce_sum x1, other arithmetic, local(): jnp.sum(jnp.where(jnp.arange(orient_logprior.shape[0])[:, None] == ref_or...  0.79 us
  transfers between devices with their start and end apart: 8, of which 6 were waited for; matrix products, arithmetic and copies ran while one was open for 13% of the time, Pallas kernels for 5%

profile of v1, /device:TPU:0, one launch (start us, length us, event | category | flops | bytes accessed | tf_op | source)
XLA Modules:
  0.0 39.1 jit_solution(14582390492341582187)
XLA Ops:
  0.6 0.6 %collective-permute-start = (bf16[128,7168]{1,0:T(8,128)(2,1)}, bf16[128,7168]{1,0:T(8,128)(2,1)S(1)}, u32[]{:S(2)}, u32[]{:S(2)}) collective-permute-start(bf16[128,7168]{1,0:T(8,128)(2,1)} %own_ref.3), channel_id=1, source_target_pairs={{0,8},{8,0},{16,24},{24,16},{1,9},{9,1},{17,25},{25,17},{2,10},{10... | collective-permute-start | bytes 5505032 | tf_op jit(solution)/shard_map/ppermute | solution.py:246
  1.2 2.6 %collective-permute-start.1 = (bf16[16,7168]{1,0:T(8,128)(2,1)}, bf16[16,7168]{1,0:T(8,128)(2,1)S(1)}, u32[]{:S(2)}, u32[]{:S(2)}) collective-permute-start(bf16[16,7168]{1,0:T(8,128)(2,1)} %refs_2_.1), channel_id=1, source_target_pairs={{0,16},{8,24},{16,0},{24,8},{1,17},{9,25},{17,1},{25,9},{2,18},{10... | collective-permute-start | bytes 688136 | tf_op jit(solution)/shard_map/ppermute | solution.py:246
  3.7 0.8 %fusion.2 = (s32[128]{0:T(128)S(1)}, s32[128]{0:T(128)S(1)}) fusion(s32[512]{0:T(512)} %param.13, s32[]{:T(128)S(6)} %select_n.69, s32[]{:T(128)S(6)} %select_n.70), kind=kLoop, calls=%fused_computation.25 | loop fusion | bytes 2056 | tf_op jit(solution)/shard_map/dynamic_slice | solution.py:269
  4.6 0.1 copy.21.class_ref
  4.7 0.7 %broadcast_in_dim.43.weight_ref = f32[1,3584]{1,0:T(1,128)S(1)} reshape(f32[3584]{0:T(1024)} %param.12) | data formatting | bytes 28672 | tf_op jit(solution)/shard_map/broadcast_in_dim | solution.py:252
  5.5 0.7 %convert_bitcast_fusion = f32[16,1]{0,1:T(1,128)S(1)} fusion(s32[16]{0:T(128)} %param.10), kind=kLoop, calls=%fused_computation.24 | loop fusion | flops 16 | bytes 128 | tf_op jit(solution)/shard_map/broadcast_in_dim | solution.py:274
  6.1 0.1 copy.22.tag_ref
  6.2 0.8 %select_reduce_fusion.1 = f32[512]{0:T(512)S(1)} fusion(f32[8]{0:T(128)} %param.15, s32[512]{0:T(512)} %param.13), kind=kLoop, calls=%fused_computation.14 | loop fusion | flops 11776 | bytes 4128 | tf_op jit(solution)/shard_map/reduce_sum | solution.py:253
  7.0 0.8 %select_reduce_fusion = f32[512]{0:T(512)S(1)} fusion(f32[64]{0:T(128)} %param.16, s32[512]{0:T(512)} %param.14), kind=kLoop, calls=%fused_computation.2 | loop fusion | flops 97792 | bytes 4352 | tf_op jit(solution)/shard_map/reduce_sum | solution.py:257
  7.8 0.1 fusion.3
  7.9 0.0 collective-permute-done.peer_ref
  7.9 0.0 copy-start
  7.9 1.5 %copy-done = bf16[128,7168]{1,0:T(8,128)(2,1)S(1)} copy-done((bf16[128,7168]{1,0:T(8,128)(2,1)S(1)}, bf16[128,7168]{1,0:T(8,128)(2,1)}, u32[]{:S(2)}) %copy-start) | copy-done | bytes 1835032
  9.4 0.0 copy-start.1
  9.4 0.9 %copy-done.1 = f32[8,3584]{1,0:T(8,128)S(1)} copy-done((f32[8,3584]{1,0:T(8,128)S(1)}, f32[8,3584]{1,0:T(8,128)}, u32[]{:S(2)}) %copy-start.1) | copy-done | bytes 114712
  10.3 0.0 copy-start.3
  10.3 0.9 %copy-done.3 = bf16[16,7168]{1,0:T(8,128)(2,1)S(1)} copy-done((bf16[16,7168]{1,0:T(8,128)(2,1)S(1)}, bf16[16,7168]{1,0:T(8,128)(2,1)}, u32[]{:S(2)}) %copy-start.3) | copy-done | bytes 229400
  11.2 0.0 copy-start.2
  11.2 2.1 %score_own.1 = (f32[9,16,256]{2,1,0:T(8,128)S(1)}, f32[16,128]{1,0:T(8,128)S(1)}, f32[1,256]{1,0:T(1,128)S(1)}) custom-call(bf16[128,7168]{1,0:T(8,128)(2,1)S(1)} %copy-done, bf16[128,7168]{1,0:T(8,128)(2,1)S(1)} %collective-permute-done.peer_ref, bf16[16,7168]{1,0:T(8,128)(2,1)S(1)} %copy-done.3, f32[8,3584]{1,0:T(8,128)S(1)} %copy-done.1, ...), custom_call_target="tpu_custom_call" | custom-call | flops 528482304 | bytes 3899392 | tf_op jit(solution)/shard_map/score_own/pallas_call | solution.py:126
  13.3 0.0 collective-permute-done.1.part_ref.refs_3_
  13.4 0.0 copy-done.2
  13.4 1.9 %score_other.1 = (f32[9,16,256]{2,1,0:T(8,128)S(1)}, f32[16,128]{1,0:T(8,128)S(1)}) custom-call(bf16[128,7168]{1,0:T(8,128)(2,1)S(1)} %copy-done, bf16[128,7168]{1,0:T(8,128)(2,1)S(1)} %collective-permute-done.peer_ref, bf16[16,7168]{1,0:T(8,128)(2,1)S(1)} %collective-permute-done.1.part_ref.refs_3_, f32[8,3584]{1,0:T(8,128)S(1)} %copy-done.2, ...), custom_call_target="tpu_custom_call" | custom-call | flops 528482304 | bytes 3899392 | tf_op jit(solution)/shard_map/score_other/pallas_call | solution.py:126
  15.2 0.1 collective-permute-start.3
  15.4 0.1 pad_add_fusion.1.place_ref
  15.4 3.6 %collective-permute-done.3.refs_1_ = f32[32,128]{1,0:T(8,128)S(1)} collective-permute-done((f32[32,128]{1,0:T(8,128)S(1)}, f32[32,128]{1,0:T(8,128)S(1)}, u32[]{:S(2)}, u32[]{:S(2)}) %collective-permute-start.3) | collective-permute-done | bytes 16416 | tf_op jit(solution)/shard_map/ppermute | solution.py:246
  19.0 2.2 %class_partial.1 = (f32[8,8,224]{2,1,0:T(8,128)S(1)}, f32[8,8,224]{2,1,0:T(8,128)S(1)}, f32[16,128]{1,0:T(8,128)S(1)}) custom-call(s32[3]{0:T(128)S(1)} %pad_add_fusion.1.place_ref, f32[8,3584]{1,0:T(8,128)S(1)} %copy-done.2, f32[32,128]{1,0:T(8,128)S(1)} %constant_dynamic-update-slice_fusion.refs_0_, f32[32,128]{1,0:T(8,128)S(1)} %collective-permute-done.3.refs_1_, ...), custom_call_target="tpu_custom_call" | custom-call | flops 1000000 | bytes 1000000 | tf_op jit(solution)/shard_map/class_partial/pallas_call | solution.py:224
  21.2 0.0 collective-permute-start.4
  21.2 1.3 %collective-permute-done.4 = f32[8,8,224]{2,1,0:T(8,128)S(1)} collective-permute-done((f32[8,8,224]{2,1,0:T(8,128)S(1)}, f32[8,8,224]{2,1,0:T(8,128)S(1)}, u32[]{:S(2)}, u32[]{:S(2)}) %collective-permute-start.4) | collective-permute-done | bytes 57376 | tf_op jit(solution)/shard_map/ppermute | solution.py:246
  22.6 2.6 %collective-permute-start.5 = (f32[4,8,224]{2,1,0:T(8,128)S(1)}, f32[4,8,224]{2,1,0:T(8,128)S(1)}, u32[]{:S(2)}, u32[]{:S(2)}) collective-permute-start(f32[4,8,224]{2,1,0:T(8,128)S(1)} %slice.52), channel_id=1, source_target_pairs={{0,4},{1,5},{2,6},{3,7},{4,0},{5,1},{6,2},{7,3},{8,12},{9,13},{10,... | collective-permute-start | bytes 86024 | tf_op jit(solution)/shard_map/ppermute | solution.py:246
  25.2 2.6 %collective-permute-done.5 = f32[4,8,224]{2,1,0:T(8,128)S(1)} collective-permute-done((f32[4,8,224]{2,1,0:T(8,128)S(1)}, f32[4,8,224]{2,1,0:T(8,128)S(1)}, u32[]{:S(2)}, u32[]{:S(2)}) %collective-permute-start.5) | collective-permute-done | bytes 28704 | tf_op jit(solution)/shard_map/ppermute | solution.py:246
  27.8 1.3 %collective-permute-start.6 = (f32[2,8,224]{2,1,0:T(8,128)S(1)}, f32[2,8,224]{2,1,0:T(8,128)S(1)}, u32[]{:S(2)}, u32[]{:S(2)}) collective-permute-start(f32[2,8,224]{2,1,0:T(8,128)S(1)} %slice.54), channel_id=1, source_target_pairs={{0,2},{1,3},{2,0},{3,1},{4,6},{5,7},{6,4},{7,5},{8,10},{9,11},{10,... | collective-permute-start | bytes 43016 | tf_op jit(solution)/shard_map/ppermute | solution.py:246
  29.1 2.5 %collective-permute-done.6 = f32[2,8,224]{2,1,0:T(8,128)S(1)} collective-permute-done((f32[2,8,224]{2,1,0:T(8,128)S(1)}, f32[2,8,224]{2,1,0:T(8,128)S(1)}, u32[]{:S(2)}, u32[]{:S(2)}) %collective-permute-start.6) | collective-permute-done | bytes 14368 | tf_op jit(solution)/shard_map/ppermute | solution.py:246
  31.6 1.5 %collective-permute-start.7 = (f32[1,8,224]{2,1,0:T(8,128)S(1)}, f32[1,8,224]{2,1,0:T(8,128)S(1)}, u32[]{:S(2)}, u32[]{:S(2)}) collective-permute-start(f32[1,8,224]{2,1,0:T(8,128)S(1)} %slice.56), channel_id=1, source_target_pairs={{0,1},{1,0},{2,3},{3,2},{4,5},{5,4},{6,7},{7,6},{8,9},{9,8},{10,11... | collective-permute-start | bytes 21512 | tf_op jit(solution)/shard_map/ppermute | solution.py:246
  33.1 0.5 %collective-permute-start.2 = (f32[9,16,256]{2,1,0:T(8,128)S(1)}, f32[9,16,256]{2,1,0:T(8,128)S(1)}, u32[]{:S(2)}, u32[]{:S(2)}) collective-permute-start(f32[9,16,256]{2,1,0:T(8,128)S(1)} %get-tuple-element.11), channel_id=1, source_target_pairs={{0,16},{8,24},{16,0},{24,8},{1,17},{9,25},{17,1},{25,9},{2,18},{10... | collective-permute-start | bytes 442376 | tf_op jit(solution)/shard_map/ppermute | solution.py:246
  33.7 0.1 copy.25
  33.8 1.5 %collective-permute-done.7 = f32[1,8,224]{2,1,0:T(8,128)S(1)} collective-permute-done((f32[1,8,224]{2,1,0:T(8,128)S(1)}, f32[1,8,224]{2,1,0:T(8,128)S(1)}, u32[]{:S(2)}, u32[]{:S(2)}) %collective-permute-start.7) | collective-permute-done | bytes 7200 | tf_op jit(solution)/shard_map/ppermute | solution.py:246
  35.3 0.6 %fusion.1 = f32[8,224]{1,0:T(8,128)} fusion(f32[1,8,224]{2,1,0:T(8,128)S(1)} %collective-permute-done.7, f32[2,8,224]{2,1,0:T(8,128)S(1)} %slice_add_fusion.1), kind=kLoop, calls=%fused_computation.17 | loop fusion | flops 1792 | bytes 21504 | tf_op jit(solution)/shard_map/squeeze | solution.py:297
  35.9 2.4 %collective-permute-done.2 = f32[9,16,256]{2,1,0:T(8,128)S(1)} collective-permute-done((f32[9,16,256]{2,1,0:T(8,128)S(1)}, f32[9,16,256]{2,1,0:T(8,128)S(1)}, u32[]{:S(2)}, u32[]{:S(2)}) %collective-permute-start.2) | collective-permute-done | bytes 147488 | tf_op jit(solution)/shard_map/ppermute | solution.py:246
  38.3 0.8 %fusion = f32[16,9,512]{2,0,1:T(8,128)} fusion(f32[9,16,128]{2,1,0:T(8,128)S(1)} %get-tuple-element.21, f32[9,16,128]{2,1,0:T(8,128)S(1)} %get-tuple-element.20, f32[9,16,128]{2,1,0:T(8,128)S(1)} %get-tuple-element.19, f32[9,16,128]{2,1,0:T(8,128)S(1)} %get-tuple-element.18, f32[9,16]{1,0:T(8,128)S(1)} %bitcast.21), kind=kLoop, calls=%fused_computation.1 | loop fusion | flops 294912 | bytes 590400 | tf_op jit(solution)/shard_map/transpose | solution.py:313
  (14 shorter events, 0.1 us)
Async XLA Ops:
  0.6 7.3 %collective-permute-start = (bf16[128,7168]{1,0:T(8,128)(2,1)}, bf16[128,7168]{1,0:T(8,128)(2,1)S(1)}, u32[]{:S(2)}, u32[]{:S(2)}) collective-permute-start(bf16[128,7168]{1,0:T(8,128)(2,1)} %own_ref.3), channel_id=1, source_target_pairs={{0,8},{8,0},{16,24},{24,16},{1,9},{9,1},{17,25},{25,17},{2,10},{10... | collective-permute-start | bytes 5505032 | tf_op jit(solution)/shard_map/ppermute | solution.py:246
  1.2 12.2 %collective-permute-start.1 = (bf16[16,7168]{1,0:T(8,128)(2,1)}, bf16[16,7168]{1,0:T(8,128)(2,1)S(1)}, u32[]{:S(2)}, u32[]{:S(2)}) collective-permute-start(bf16[16,7168]{1,0:T(8,128)(2,1)} %refs_2_.1), channel_id=1, source_target_pairs={{0,16},{8,24},{16,0},{24,8},{1,17},{9,25},{17,1},{25,9},{2,18},{10... | collective-permute-start | bytes 688136 | tf_op jit(solution)/shard_map/ppermute | solution.py:246
  7.9 1.5 %copy-start = (bf16[128,7168]{1,0:T(8,128)(2,1)S(1)}, bf16[128,7168]{1,0:T(8,128)(2,1)}, u32[]{:S(2)}) copy-start(bf16[128,7168]{1,0:T(8,128)(2,1)} %own_ref.3) | copy-start | bytes 5505028
  9.4 0.9 %copy-start.1 = (f32[8,3584]{1,0:T(8,128)S(1)}, f32[8,3584]{1,0:T(8,128)}, u32[]{:S(2)}) copy-start(f32[8,3584]{1,0:T(8,128)} %constant.42.clone.table_ref) | copy-start | bytes 344068
  10.3 0.9 %copy-start.3 = (bf16[16,7168]{1,0:T(8,128)(2,1)S(1)}, bf16[16,7168]{1,0:T(8,128)(2,1)}, u32[]{:S(2)}) copy-start(bf16[16,7168]{1,0:T(8,128)(2,1)} %refs_2_.1) | copy-start | bytes 688132
  11.2 2.1 %copy-start.2 = (f32[8,3584]{1,0:T(8,128)S(1)}, f32[8,3584]{1,0:T(8,128)}, u32[]{:S(2)}) copy-start(f32[8,3584]{1,0:T(8,128)} %constant.42.clone.table_ref) | copy-start | bytes 344068
  15.2 3.8 %collective-permute-start.3 = (f32[32,128]{1,0:T(8,128)S(1)}, f32[32,128]{1,0:T(8,128)S(1)}, u32[]{:S(2)}, u32[]{:S(2)}) collective-permute-start(f32[32,128]{1,0:T(8,128)S(1)} %constant_dynamic-update-slice_fusion.refs_0_), channel_id=1, source_target_pairs={{0,16},{8,24},{16,0},{24,8},{1,17},{9,25},{17,1},{25,9},{2,18},{10... | collective-permute-start | bytes 49160 | tf_op jit(solution)/shard_map/ppermute | solution.py:246
  21.2 1.3 %collective-permute-start.4 = (f32[8,8,224]{2,1,0:T(8,128)S(1)}, f32[8,8,224]{2,1,0:T(8,128)S(1)}, u32[]{:S(2)}, u32[]{:S(2)}) collective-permute-start(f32[8,8,224]{2,1,0:T(8,128)S(1)} %get-tuple-element.17), channel_id=1, source_target_pairs={{0,8},{8,0},{16,24},{24,16},{1,9},{9,1},{17,25},{25,17},{2,10},{10... | collective-permute-start | bytes 172040 | tf_op jit(solution)/shard_map/ppermute | solution.py:246
  22.6 5.2 %collective-permute-start.5 = (f32[4,8,224]{2,1,0:T(8,128)S(1)}, f32[4,8,224]{2,1,0:T(8,128)S(1)}, u32[]{:S(2)}, u32[]{:S(2)}) collective-permute-start(f32[4,8,224]{2,1,0:T(8,128)S(1)} %slice.52), channel_id=1, source_target_pairs={{0,4},{1,5},{2,6},{3,7},{4,0},{5,1},{6,2},{7,3},{8,12},{9,13},{10,... | collective-permute-start | bytes 86024 | tf_op jit(solution)/shard_map/ppermute | solution.py:246
  27.8 3.8 %collective-permute-start.6 = (f32[2,8,224]{2,1,0:T(8,128)S(1)}, f32[2,8,224]{2,1,0:T(8,128)S(1)}, u32[]{:S(2)}, u32[]{:S(2)}) collective-permute-start(f32[2,8,224]{2,1,0:T(8,128)S(1)} %slice.54), channel_id=1, source_target_pairs={{0,2},{1,3},{2,0},{3,1},{4,6},{5,7},{6,4},{7,5},{8,10},{9,11},{10,... | collective-permute-start | bytes 43016 | tf_op jit(solution)/shard_map/ppermute | solution.py:246
  31.6 3.7 %collective-permute-start.7 = (f32[1,8,224]{2,1,0:T(8,128)S(1)}, f32[1,8,224]{2,1,0:T(8,128)S(1)}, u32[]{:S(2)}, u32[]{:S(2)}) collective-permute-start(f32[1,8,224]{2,1,0:T(8,128)S(1)} %slice.56), channel_id=1, source_target_pairs={{0,1},{1,0},{2,3},{3,2},{4,5},{5,4},{6,7},{7,6},{8,9},{9,8},{10,11... | collective-permute-start | bytes 21512 | tf_op jit(solution)/shard_map/ppermute | solution.py:246
  33.1 5.1 %collective-permute-start.2 = (f32[9,16,256]{2,1,0:T(8,128)S(1)}, f32[9,16,256]{2,1,0:T(8,128)S(1)}, u32[]{:S(2)}, u32[]{:S(2)}) collective-permute-start(f32[9,16,256]{2,1,0:T(8,128)S(1)} %get-tuple-element.11), channel_id=1, source_target_pairs={{0,16},{8,24},{16,0},{24,8},{1,17},{9,25},{17,1},{25,9},{2,18},{10... | collective-permute-start | bytes 442376 | tf_op jit(solution)/shard_map/ppermute | solution.py:246

commit v2 on v1

v2 whole, which is shorter than its diff:
```python
import functools
import math

import jax
import jax.numpy as jnp
import numpy as np
from jax import lax
from jax.experimental import pallas as pl
from jax.experimental.pallas import tpu as pltpu
from jax.sharding import PartitionSpec as P

SHIFTS = 9
PAIRS = 4
LANES = 128
CHUNK = 512
VMEM_LIMIT = 24 * 1024 * 1024


def turning_table(count):
    coeffs = np.arange(count)
    column_freq = (coeffs % 56).astype(np.float32)
    row_freq = (coeffs // 56 - 32).astype(np.float32)
    shift_ids = np.arange(SHIFTS - PAIRS, SHIFTS)
    right = (shift_ids % 3 - 1).astype(np.float32)
    down = (shift_ids // 3 - 1).astype(np.float32)
    turning = np.float32(2.0 * math.pi / 96.0) * (
        right[:, None] * column_freq[None, :] + down[:, None] * row_freq[None, :]
    )
    return np.concatenate([np.cos(turning), np.sin(turning)], axis=0).astype(np.float32)


def chunks(total):
    size = CHUNK if total % CHUNK == 0 else LANES
    return [(start, size) for start in range(0, total, size)]


def dot_nt(left, right):
    return lax.dot_general(
        left, right, (((1,), (1,)), ((), ())), preferred_element_type=jnp.float32
    )


def two_parts(value):
    high = value.astype(jnp.bfloat16)
    low = (value - high.astype(jnp.float32)).astype(jnp.bfloat16)
    return [high, low]


def cross_terms(ref_blocks, part_ref, table_ref, weight_ref, want_norm, arriving=()):
    rows, width = part_ref.shape
    coefs = width // 2
    count = sum(block.shape[0] for block in ref_blocks)
    cross = jnp.zeros((SHIFTS * rows, count), jnp.float32)
    norm = jnp.zeros((count, LANES), jnp.float32)
    middle = SHIFTS // 2
    for i, (start, size) in enumerate(chunks(coefs)):
        for copy in arriving[i] if arriving else ():
            copy.wait()
        re = pl.ds(start, size)
        im = pl.ds(coefs + start, size)
        row = start // LANES
        weight = jnp.concatenate(
            [weight_ref[row + j : row + j + 1, :] for j in range(size // LANES)], axis=1
        )
        twice = 2.0 * weight
        table = table_ref[:, re] * twice
        x = part_ref[:, re].astype(jnp.float32)
        y = part_ref[:, im].astype(jnp.float32)
        real = [None] * SHIFTS
        imag = [None] * SHIFTS
        real[middle] = (x * twice).astype(jnp.bfloat16)
        imag[middle] = (y * twice).astype(jnp.bfloat16)
        for p in range(PAIRS):
            cosine = table[p : p + 1]
            sine = table[PAIRS + p : PAIRS + p + 1]
            xc, ys, xs, yc = x * cosine, y * sine, x * sine, y * cosine
            t = middle + 1 + p
            real[t] = (xc - ys).astype(jnp.bfloat16)
            imag[t] = (xs + yc).astype(jnp.bfloat16)
            real[SHIFTS - 1 - t] = (xc + ys).astype(jnp.bfloat16)
            imag[SHIFTS - 1 - t] = (yc - xs).astype(jnp.bfloat16)
        refs_re = jnp.concatenate([block[:, re] for block in ref_blocks], axis=0)
        refs_im = jnp.concatenate([block[:, im] for block in ref_blocks], axis=0)
        cross += dot_nt(jnp.concatenate(real, axis=0), refs_re)
        cross += dot_nt(jnp.concatenate(imag, axis=0), refs_im)
        if want_norm:
            for lane in range(0, size, LANES):
                a = refs_re[:, lane : lane + LANES].astype(jnp.float32)
                b = refs_im[:, lane : lane + LANES].astype(jnp.float32)
                norm += weight[:, lane : lane + LANES] * (a * a + b * b)
    return cross, norm


def block_prior(index, class_ref, orient_ref, class_prior_ref, orient_prior_ref):
    kind = class_ref[pl.ds(index, 1), :]
    orient = orient_ref[pl.ds(index, 1), :]
    first = jnp.zeros(kind.shape, jnp.float32)
    second = jnp.zeros(kind.shape, jnp.float32)
    for c in range(class_prior_ref.shape[0]):
        first = jnp.where(kind == c, class_prior_ref[c], first)
    for o in range(orient_prior_ref.shape[0]):
        second = jnp.where(orient == o, orient_prior_ref[o], second)
    return first + second


def statistics(classes, me, blocks, class_ref, tag):
    scores = jnp.concatenate(blocks, axis=1)
    rows = scores.shape[0] // SHIFTS
    peak = scores[:rows]
    for t in range(1, SHIFTS):
        peak = jnp.maximum(peak, scores[t * rows : (t + 1) * rows])
    peak = jnp.max(peak, axis=1, keepdims=True)
    mass = jnp.exp(scores - jnp.concatenate([peak] * SHIFTS, axis=0))
    kind = jnp.concatenate(
        [class_ref[pl.ds(me, 1), :], class_ref[pl.ds(lax.bitwise_xor(me, 1), 1), :]], axis=1
    )
    want = lax.rem(lax.broadcasted_iota(jnp.int32, (LANES, scores.shape[1]), 0), classes)
    table = jnp.where(want == kind, 1.0, 0.0).astype(jnp.bfloat16)
    span = SHIFTS * rows
    by_class = dot_nt(jnp.concatenate(two_parts(mass), axis=0), table)
    by_class = by_class[:span] + by_class[span:]
    lane = lax.broadcasted_iota(jnp.int32, (rows, LANES), 1)
    shift = lane // classes
    stats = jnp.where(lane == SHIFTS * classes, peak, 0.0)
    if tag is not None:
        stats = jnp.where(lane == SHIFTS * classes + 1, tag, stats)
    for t in range(SHIFTS):
        stats = jnp.where(shift == t, by_class[t * rows : (t + 1) * rows], stats)
    return stats


def near_body(classes, refs_hbm, part_hbm, table_hbm, weight_hbm, class_hbm, orient_hbm,
              class_prior_hbm, orient_prior_hbm, offset_hbm, scores_ref, bias_ref, tag_ref,
              refs_ref, part_ref, table_ref, weight_ref, class_ref,
              orient_ref, class_prior_ref, orient_prior_ref, offset_ref, small_sems, refs_sems):
    me = lax.axis_index("ref")
    coefs = part_ref.shape[1] // 2
    small = [
        pltpu.make_async_copy(source, target, small_sems.at[i])
        for i, (source, target) in enumerate(
            [
                (part_hbm, part_ref), (table_hbm, table_ref), (weight_hbm, weight_ref),
                (class_hbm, class_ref), (orient_hbm, orient_ref),
                (class_prior_hbm, class_prior_ref), (orient_prior_hbm, orient_prior_ref),
                (offset_hbm, offset_ref),
            ]
        )
    ]
    for copy in small:
        copy.start()
    arriving = []
    for i, (start, size) in enumerate(chunks(coefs)):
        pair = []
        for j in range(2):
            columns = pl.ds(j * coefs + start, size)
            pair.append(
                pltpu.make_async_copy(
                    refs_hbm.at[:, columns], refs_ref.at[:, columns], refs_sems.at[2 * i + j]
                )
            )
        for copy in pair:
            copy.start()
        arriving.append(pair)
    for copy in small:
        copy.wait()
    rows = part_ref.shape[0]
    row = lax.broadcasted_iota(jnp.int32, (rows, LANES), 0)
    tag = jnp.zeros((rows, LANES), jnp.int32)
    for i in range(rows):
        tag = jnp.where(row == i, offset_ref[i], tag)
    tag_ref[...] = tag.astype(jnp.float32)
    cross, norm = cross_terms([refs_ref], part_ref, table_ref, weight_ref, True, arriving)
    priors = [
        block_prior(
            lax.bitwise_xor(me, i), class_ref, orient_ref, class_prior_ref, orient_prior_ref
        )
        for i in range(2)
    ]
    bias = priors[0] - jnp.sum(jnp.transpose(norm), axis=0, keepdims=True)
    bias_ref[0:1, :] = bias
    bias_ref[1:2, :] = priors[1]
    scores_ref[...] = (cross + bias).reshape(scores_ref.shape)


def pair_body(classes, near_ref, peer_ref, part_ref, table_ref, weight_ref, class_ref, prior_ref,
              tag_ref, scores_ref, bias_ref, stats_ref):
    me = lax.axis_index("ref")
    cross, norm = cross_terms([peer_ref], part_ref, table_ref, weight_ref, True)
    bias = prior_ref[1:2, :] - jnp.sum(jnp.transpose(norm), axis=0, keepdims=True)
    bias_ref[0:1, :] = prior_ref[0:1, :]
    bias_ref[1:2, :] = bias
    scores = cross + bias
    scores_ref[...] = scores.reshape(scores_ref.shape)
    near = near_ref[...].reshape(scores.shape)
    stats_ref[...] = statistics(classes, me, [near, scores], class_ref, tag_ref[...])


def far_body(classes, own_ref, peer_ref, part_ref, table_ref, weight_ref, class_ref, bias_ref,
             scores_ref, stats_ref):
    me = lax.axis_index("ref")
    block = own_ref.shape[0]
    cross, _ = cross_terms([own_ref, peer_ref], part_ref, table_ref, weight_ref, False)
    blocks = [cross[:, i * block : (i + 1) * block] + bias_ref[i : i + 1, :] for i in range(2)]
    stats_ref[...] = statistics(classes, me, blocks, class_ref, None)
    for i in range(2):
        scores_ref[:, :, i * block : (i + 1) * block] = blocks[i].reshape(
            scores_ref.shape[0], scores_ref.shape[1], block
        )


VMEM = pl.BlockSpec(memory_space=pltpu.VMEM)
HBM = pl.BlockSpec(memory_space=pltpu.HBM)


def call(body, name, shapes, specs, cost, *operands, scratch=()):
    return pl.pallas_call(
        body,
        out_shape=[
            shape if isinstance(shape, jax.ShapeDtypeStruct)
            else jax.ShapeDtypeStruct(shape, jnp.float32)
            for shape in shapes
        ],
        scratch_shapes=scratch,
        in_specs=specs,
        out_specs=[VMEM] * len(shapes),
        name=name,
        compiler_params=pltpu.CompilerParams(vmem_limit_bytes=VMEM_LIMIT),
        cost_estimate=pl.CostEstimate(
            flops=int(cost * 5e8), bytes_accessed=int(cost * 1e6), transcendentals=0
        ),
    )(*operands)


def sums_body(groups, classes, scale, table_ref, *refs):
    stats = refs[:groups]
    parts = refs[groups : 2 * groups]
    sums_ref, total_ref = refs[2 * groups :]
    rows = parts[0].shape[0]
    width = parts[0].shape[1]
    coefs = width // 2
    span = width // groups
    used = SHIFTS * classes
    me = lax.axis_index("ref")
    dom = lax.axis_index("dom")
    chip, core = me // 2, lax.rem(me, 2)
    lane = lax.broadcasted_iota(jnp.int32, (rows, LANES), 1)
    shift = lane // classes
    right = (shift % 3 - 1).astype(jnp.float32)
    down = (shift // 3 - 1).astype(jnp.float32)
    posts = []
    for slot in range(groups):
        seen = [stats[i][(slot ^ i) * rows : ((slot ^ i) + 1) * rows] for i in range(groups)]
        peaks = [value[:, used : used + 1] for value in seen]
        peak = functools.reduce(jnp.maximum, peaks)
        mass = sum(value * jnp.exp(low - peak) for value, low in zip(seen, peaks))
        centre = stats[slot][:rows, used + 1 : used + 2].astype(jnp.int32)
        across = right - (centre % 3 - 1).astype(jnp.float32)
        along = down - (centre // 3 - 1).astype(jnp.float32)
        prior = -0.5 * (across * across + along * along)
        mass = jnp.where(lane < used, mass * jnp.exp(prior), 0.0)
        whole = jnp.sum(mass, axis=1, keepdims=True)
        posts.append(mass / whole)
        if slot == 0:
            total_ref[...] = prior - (peak + jnp.log(whole))
    post = jnp.transpose(jnp.concatenate(posts, axis=0)) * scale
    middle = SHIFTS // 2
    by_shift = [post[t * classes : (t + 1) * classes] for t in range(SHIFTS)]
    even = [by_shift[middle]]
    odd = []
    sign = jnp.where(chip < groups // 2, -1.0, 1.0)
    for p in range(PAIRS):
        t = middle + 1 + p
        even.append(by_shift[t] + by_shift[SHIFTS - 1 - t])
        odd.append(sign * (by_shift[t] - by_shift[SHIFTS - 1 - t]))
    even = jnp.concatenate(two_parts(jnp.concatenate(even, axis=0)), axis=0)
    odd = jnp.concatenate(two_parts(jnp.concatenate(odd, axis=0)), axis=0)
    column = chip * span
    other = lax.rem(column + coefs, width)
    base = lax.rem(column, coefs)
    step = CHUNK if span % CHUNK == 0 else LANES
    ne = (PAIRS + 1) * classes
    no = PAIRS * classes
    pieces = []
    for start in range(0, span, step):
        u = jnp.concatenate(
            [part[:, pl.ds(pl.multiple_of(column + start, LANES), step)] for part in parts], axis=0
        )
        v = jnp.concatenate(
            [part[:, pl.ds(pl.multiple_of(other + start, LANES), step)] for part in parts], axis=0
        )
        table = table_ref[:, pl.ds(pl.multiple_of(base + start, LANES), step)]
        evens = jnp.dot(even, u, preferred_element_type=jnp.float32)
        odds = jnp.dot(odd, v, preferred_element_type=jnp.float32)
        evens = evens[:ne] + evens[ne:]
        odds = odds[:no] + odds[no:]
        result = evens[:classes]
        for p in range(PAIRS):
            result += table[p : p + 1] * evens[(p + 1) * classes : (p + 2) * classes]
            result += table[PAIRS + p : PAIRS + p + 1] * odds[p * classes : (p + 1) * classes]
        pieces.append(result)
    result = jnp.concatenate(pieces, axis=1)
    slots = sums_ref.shape[1]
    columns = sums_ref.shape[3]
    for half in range(2):
        for d in range(slots):
            at = (half * slots + d) * columns
            sums_ref[lax.bitwise_xor(core, half), lax.bitwise_xor(dom, d)] = result[
                :, at : at + columns
            ]


def order_body(block, groups, total_ref, *refs):
    out_ref = refs[-1]
    me = lax.axis_index("ref")
    slot = 0
    for ref in refs[:-1]:
        for at in range(0, ref.shape[2], block):
            place = pl.multiple_of(lax.bitwise_xor(me, slot) * block, LANES)
            for t in range(SHIFTS):
                lift = total_ref[:, t * groups : t * groups + 1]
                out_ref[t, :, pl.ds(place, block)] = ref[t, :, at : at + block] + lift
            slot += 1


def local(refs_axis, dom_axis, particles, offsets, references, noise_weight, ref_class, ref_orient,
          class_logprior, orient_logprior):
    rows, width = particles.shape
    coefs = width // 2
    block = references.shape[0]
    classes = class_logprior.shape[0]
    groups = refs_axis // 2
    me = lax.axis_index("ref")

    def swap(value, axis, size, bit):
        return lax.ppermute(value, axis, [(i, i ^ bit) for i in range(size)])

    with jax.named_scope("particles"):
        others = [swap(particles, "ref", refs_axis, 2 * i) for i in range(1, groups)]
    with jax.named_scope("references"):
        peer_refs = swap(references, "ref", refs_axis, 1)

    table = jnp.asarray(turning_table(coefs))
    weight = noise_weight.reshape(coefs // LANES, LANES)
    kinds = ref_class.reshape(refs_axis, block)
    orients = ref_orient.reshape(refs_axis, block)
    loaded = [references, particles, table, weight, kinds]
    near, prior, tag, *held = call(
        functools.partial(near_body, classes),
        "score_near",
        [(SHIFTS, rows, block), (2, block), (rows, LANES)]
        + [jax.ShapeDtypeStruct(value.shape, value.dtype) for value in loaded],
        [HBM] * 9,
        1.0,
        *[pltpu.with_memory_space_constraint(v, pltpu.HBM) for v in [*loaded, orients, class_logprior, orient_logprior, offsets]],
        scratch=[
            pltpu.VMEM(orients.shape, jnp.int32),
            pltpu.SMEM(class_logprior.shape, jnp.float32),
            pltpu.SMEM(orient_logprior.shape, jnp.float32),
            pltpu.SMEM(offsets.shape, jnp.int32),
            pltpu.SemaphoreType.DMA((8,)),
            pltpu.SemaphoreType.DMA((2 * len(chunks(coefs)),)),
        ],
    )
    held_refs, held_part, table, weight, kinds = held
    shared = (table, weight, kinds)
    pair, bias, own_stats = call(
        functools.partial(pair_body, classes),
        "score_pair",
        [(SHIFTS, rows, block), (2, block), (rows, LANES)],
        [VMEM] * 8,
        1.0,
        near, peer_refs, held_part, *shared, prior, tag,
    )
    sent_scores, stats = [], [own_stats]
    for other in others:
        value, stat = call(
            functools.partial(far_body, classes),
            "score_far",
            [(SHIFTS, rows, 2 * block), (rows, LANES)],
            [VMEM] * 7,
            1.0,
            held_refs, peer_refs, other, *shared, bias,
        )
        sent_scores.append(value)
        stats.append(stat)
    stats = jnp.concatenate(stats, axis=0)
    with jax.named_scope("stats"):
        seen = [stats] + [swap(stats, "ref", refs_axis, 2 * i) for i in range(1, groups)]
    with jax.named_scope("scores"):
        got = [swap(value, "ref", refs_axis, 2 * (i + 1)) for i, value in enumerate(sent_scores)]
    devices = refs_axis * dom_axis
    with jax.named_scope("partial"):
        sums, total = call(
            functools.partial(sums_body, groups, classes, 1.0 / math.sqrt(rows * devices)),
            "class_partial",
            [(2, dom_axis, classes, width // devices), (rows, LANES)],
            [VMEM] * (1 + 2 * groups),
            1.0,
            table, *seen, held_part, *others,
        )
    with jax.named_scope("halve"):
        keep = sums[0] + swap(sums[1], "ref", refs_axis, 1)
        slots = dom_axis
        while slots > 1:
            slots //= 2
            keep = keep[:slots] + swap(keep[slots:], "dom", dom_axis, slots)
        class_sums = keep[0]

    blocks = [near, pair] + got
    if block % LANES == 0:
        with jax.named_scope("order"):
            (log_post,) = call(
                functools.partial(order_body, block, classes),
                "log_post",
                [(SHIFTS, rows, refs_axis * block)],
                [VMEM] * (1 + len(blocks)),
                0.5,
                total, *blocks,
            )
    else:
        pieces = [near, pair]
        for value in got:
            pieces += [value[:, :, :block], value[:, :, block:]]
        bit = 1
        while bit < refs_axis:
            pieces = [
                jnp.where((me & bit) != 0, pieces[j ^ bit], pieces[j]) for j in range(refs_axis)
            ]
            bit *= 2
        lift = total[:, : SHIFTS * classes : classes].T
        log_post = jnp.concatenate(pieces, axis=2) + lift[:, :, None]
    return (jnp.transpose(log_post, (1, 0, 2)), class_sums)


def solution(mesh):
    return jax.shard_map(
        functools.partial(local, mesh.shape["ref"], mesh.shape["dom"]),
        mesh=mesh,
        in_specs=(
            P(("ref", "dom"), None),
            P(("ref", "dom")),
            P("ref", None),
            P(),
            P(),
            P(),
            P(),
            P(),
        ),
        out_specs=(P(("ref", "dom"), None, None), P(None, ("ref", "dom"))),
        check_vma=False,
    )
```

time: 39.5 us -> 34.9 us (0.88)
  local copies, waits for them, and re-layouts: 5.32 us -> 0.03 us
  starting transfers between devices: 9.22 us -> 13.4 us
  other arithmetic: 3.79 us -> 0.62 us
  waiting for transfers between devices: 13.9 us -> 11.5 us
  Pallas kernels: 6.13 us -> 8.4 us
    ppermute x8, starting transfers between devices: 9.22 us -> 13.4 us  [swap(): return lax.ppermute(value, axis, [(i, i ^ bit) for i in range(size)])]
    unnamed x9 -> x1, local copies, waits for them, and re-layouts: 3.34 us -> 0.01 us
    ppermute x8, waiting for transfers between devices: 13.9 us -> 11.5 us  [swap(): return lax.ppermute(value, axis, [(i, i ^ bit) for i in range(size)])]
    pallas_call x3 -> x5, Pallas kernels: 6.13 us -> 8.4 us  [call(): pl.pallas_call(body, out_shape=[shape if isinstance(shape, jax.ShapeDtype...]
    reduce_sum x2 -> x0, other arithmetic: 1.57 us -> none  [the longest x1 0.79 us: local(): jnp.sum(jnp.where(jnp.arange(orient_logprior.shape[0])[:, None] == ref_or...]
    broadcast_in_dim x3 -> x0, local copies, waits for them, and re-layouts: 0.96 us -> none  [the longest x1 0.73 us: local(): weight = noise_weight[None, :]]
    dynamic_slice x2 -> x0, local copies, waits for them, and re-layouts: 0.91 us -> none  [mine(): lax.dynamic_slice(row, ((me ^ i) * block,), (block,))]
    transpose x1 -> x0, other arithmetic: 0.81 us -> none  [local(): return (jnp.transpose(log_post, (1, 0, 2)), class_sums)]
  transfers between devices with their start and end apart: 8 -> 8, of which waited for: 6 -> 7; matrix products, arithmetic and copies ran while one was open for 13% -> 2% of each run, Pallas kernels for 5% -> 14%
where the time goes in v2:
time: 34.9 us; the launch traced here: 34.7 us
  starting transfers between devices  13.4 us (38%)
  waiting for transfers between devices  11.5 us (33%)
  Pallas kernels  8.4 us (24%)
  between operations  0.72 us (2%)
  other arithmetic  0.62 us (2%)
    ppermute x8, starting transfers between devices, swap(): return lax.ppermute(value, axis, [(i, i ^ bit) for i in range(size)])  13.4 us
    ppermute x8, waiting for transfers between devices, swap(): return lax.ppermute(value, axis, [(i, i ^ bit) for i in range(size)])  11.5 us
    pallas_call x5, Pallas kernels, call(): pl.pallas_call(body, out_shape=[shape if isinstance(shape, jax.ShapeDtype...  8.4 us
  transfers between devices with their start and end apart: 8, of which 7 were waited for; matrix products, arithmetic and copies ran while one was open for 2% of the time, Pallas kernels for 14%

profile of v2, /device:TPU:0, one launch (start us, length us, event | category | flops | bytes accessed | tf_op | source)
XLA Modules:
  0.0 34.7 jit_solution(17181586192456464760)
XLA Ops:
  0.6 0.6 %collective-permute-start = (bf16[128,7168]{1,0:T(8,128)(2,1)}, bf16[128,7168]{1,0:T(8,128)(2,1)S(1)}, u32[]{:S(2)}, u32[]{:S(2)}) collective-permute-start(bf16[128,7168]{1,0:T(8,128)(2,1)} %refs_hbm.1), channel_id=1, source_target_pairs={{0,8},{8,0},{16,24},{24,16},{1,9},{9,1},{17,25},{25,17},{2,10},{10... | collective-permute-start | bytes 5505032 | tf_op jit(solution)/shard_map/references/ppermute | solution.py:335
  1.2 2.6 %collective-permute-start.1 = (bf16[16,7168]{1,0:T(8,128)(2,1)}, bf16[16,7168]{1,0:T(8,128)(2,1)S(1)}, u32[]{:S(2)}, u32[]{:S(2)}) collective-permute-start(bf16[16,7168]{1,0:T(8,128)(2,1)} %part_hbm.1), channel_id=1, source_target_pairs={{0,16},{8,24},{16,0},{24,8},{1,17},{9,25},{17,1},{25,9},{2,18},{10... | collective-permute-start | bytes 688136 | tf_op jit(solution)/shard_map/particles/ppermute | solution.py:335
  3.7 3.5 %score_near.1 = (f32[9,16,128]{2,1,0:T(8,128)S(1)}, f32[2,128]{1,0:T(2,128)S(1)}, f32[16,128]{1,0:T(8,128)S(1)}, bf16[128,7168]{1,0:T(8,128)(2,1)S(1)}, bf16[16,...) custom-call(bf16[128,7168]{1,0:T(8,128)(2,1)} %refs_hbm.1, ...), custom_call_target="tpu_custom_call" | custom-call | flops 500000000 | bytes 1000000 | tf_op jit(solution)/shard_map/score_near/pallas_call | solution.py:216
  7.3 0.0 collective-permute-done.peer_ref
  7.3 1.5 %score_pair.1 = (f32[9,16,128]{2,1,0:T(8,128)S(1)}, f32[2,128]{1,0:T(2,128)S(1)}, f32[16,128]{1,0:T(8,128)S(1)}) custom-call(f32[9,16,128]{2,1,0:T(8,128)S(1)} %get-tuple-element.18.near_ref.refs_0_, bf16[128,7168]{1,0:T(8,128)(2,1)S(1)} %collective-permute-done.peer_ref, bf16[16,7168]{1,0:T(8,128)(2,1)S(1)} %get-tuple-element.19.part_ref.refs_2_, ...), custom_call_target="tpu_custom_call" | custom-call | flops 500000000 | bytes 1000000 | tf_op jit(solution)/shard_map/score_pair/pallas_call | solution.py:216
  8.8 1.4 %collective-permute-done.1.part_ref.refs_3_ = bf16[16,7168]{1,0:T(8,128)(2,1)S(1)} collective-permute-done((bf16[16,7168]{1,0:T(8,128)(2,1)}, bf16[16,7168]{1,0:T(8,128)(2,1)S(1)}, u32[]{:S(2)}, u32[]{:S(2)}) %collective-permute-start.1) | collective-permute-done | bytes 229408 | tf_op jit(solution)/shard_map/particles/ppermute | solution.py:335
  10.2 1.8 %score_far.1 = (f32[9,16,256]{2,1,0:T(8,128)S(1)}, f32[16,128]{1,0:T(8,128)S(1)}) custom-call(bf16[128,7168]{1,0:T(8,128)(2,1)S(1)} %get-tuple-element.25.own_ref, bf16[128,7168]{1,0:T(8,128)(2,1)S(1)} %collective-permute-done.peer_ref, bf16[16,7168]{1,0:T(8,128)(2,1)S(1)} %collective-permute-done.1.part_ref.refs_3_, ...), custom_call_target="tpu_custom_call" | custom-call | flops 500000000 | bytes 1000000 | tf_op jit(solution)/shard_map/score_far/pallas_call | solution.py:216
  11.9 1.8 %collective-permute-start.2 = (f32[32,128]{1,0:T(8,128)S(1)}, f32[32,128]{1,0:T(8,128)S(1)}, u32[]{:S(2)}, u32[]{:S(2)}) collective-permute-start(f32[32,128]{1,0:T(8,128)S(1)} %constant_dynamic-update-slice_fusion.refs_0_), channel_id=1, source_target_pairs={{0,16},{8,24},{16,0},{24,8},{1,17},{9,25},{17,1},{25,9},{2,18},{10... | collective-permute-start | bytes 49160 | tf_op jit(solution)/shard_map/stats/ppermute | solution.py:335
  13.8 2.0 %collective-permute-done.2.refs_1_ = f32[32,128]{1,0:T(8,128)S(1)} collective-permute-done((f32[32,128]{1,0:T(8,128)S(1)}, f32[32,128]{1,0:T(8,128)S(1)}, u32[]{:S(2)}, u32[]{:S(2)}) %collective-permute-start.2) | collective-permute-done | bytes 16416 | tf_op jit(solution)/shard_map/stats/ppermute | solution.py:335
  15.8 0.7 %class_partial.1 = (f32[2,8,8,224]{3,2,1,0:T(8,128)S(1)}, f32[16,128]{1,0:T(8,128)S(1)}) custom-call(f32[8,3584]{1,0:T(8,128)S(1)} %get-tuple-element.17.table_ref, f32[32,128]{1,0:T(8,128)S(1)} %constant_dynamic-update-slice_fusion.refs_0_, f32[32,128]{1,0:T(8,128)S(1)} %collective-permute-done.2.refs_1_, ...), custom_call_target="tpu_custom_call" | custom-call | flops 500000000 | bytes 1000000 | tf_op jit(solution)/shard_map/partial/class_partial/pallas_call | solution.py:216
  16.5 0.1 collective-permute-start.4
  16.6 1.2 %collective-permute-done.4 = f32[8,8,224]{2,1,0:T(8,128)S(1)} collective-permute-done((f32[8,8,224]{2,1,0:T(8,128)S(1)}, f32[8,8,224]{2,1,0:T(8,128)S(1)}, u32[]{:S(2)}, u32[]{:S(2)}) %collective-permute-start.4) | collective-permute-done | bytes 57376 | tf_op jit(solution)/shard_map/halve/ppermute | solution.py:335
  17.8 2.9 %collective-permute-start.5 = (f32[4,8,224]{2,1,0:T(8,128)S(1)}, f32[4,8,224]{2,1,0:T(8,128)S(1)}, u32[]{:S(2)}, u32[]{:S(2)}) collective-permute-start(f32[4,8,224]{2,1,0:T(8,128)S(1)} %slice.33), channel_id=1, source_target_pairs={{0,4},{1,5},{2,6},{3,7},{4,0},{5,1},{6,2},{7,3},{8,12},{9,13},{10,... | collective-permute-start | bytes 86024 | tf_op jit(solution)/shard_map/halve/ppermute | solution.py:335
  20.7 2.0 %collective-permute-done.5 = f32[4,8,224]{2,1,0:T(8,128)S(1)} collective-permute-done((f32[4,8,224]{2,1,0:T(8,128)S(1)}, f32[4,8,224]{2,1,0:T(8,128)S(1)}, u32[]{:S(2)}, u32[]{:S(2)}) %collective-permute-start.5) | collective-permute-done | bytes 28704 | tf_op jit(solution)/shard_map/halve/ppermute | solution.py:335
  22.7 1.9 %collective-permute-start.6 = (f32[2,8,224]{2,1,0:T(8,128)S(1)}, f32[2,8,224]{2,1,0:T(8,128)S(1)}, u32[]{:S(2)}, u32[]{:S(2)}) collective-permute-start(f32[2,8,224]{2,1,0:T(8,128)S(1)} %slice.35), channel_id=1, source_target_pairs={{0,2},{1,3},{2,0},{3,1},{4,6},{5,7},{6,4},{7,5},{8,10},{9,11},{10,... | collective-permute-start | bytes 43016 | tf_op jit(solution)/shard_map/halve/ppermute | solution.py:335
  24.6 1.9 %collective-permute-done.6 = f32[2,8,224]{2,1,0:T(8,128)S(1)} collective-permute-done((f32[2,8,224]{2,1,0:T(8,128)S(1)}, f32[2,8,224]{2,1,0:T(8,128)S(1)}, u32[]{:S(2)}, u32[]{:S(2)}) %collective-permute-start.6) | collective-permute-done | bytes 14368 | tf_op jit(solution)/shard_map/halve/ppermute | solution.py:335
  26.5 2.1 %collective-permute-start.7 = (f32[1,8,224]{2,1,0:T(8,128)S(1)}, f32[1,8,224]{2,1,0:T(8,128)S(1)}, u32[]{:S(2)}, u32[]{:S(2)}) collective-permute-start(f32[1,8,224]{2,1,0:T(8,128)S(1)} %slice.37), channel_id=1, source_target_pairs={{0,1},{1,0},{2,3},{3,2},{4,5},{5,4},{6,7},{7,6},{8,9},{9,8},{10,11... | collective-permute-start | bytes 21512 | tf_op jit(solution)/shard_map/halve/ppermute | solution.py:335
  28.7 1.5 %collective-permute-start.3 = (f32[9,16,256]{2,1,0:T(8,128)S(1)}, f32[9,16,256]{2,1,0:T(8,128)S(1)}, u32[]{:S(2)}, u32[]{:S(2)}) collective-permute-start(f32[9,16,256]{2,1,0:T(8,128)S(1)} %get-tuple-element.30), channel_id=1, source_target_pairs={{0,16},{8,24},{16,0},{24,8},{1,17},{9,25},{17,1},{25,9},{2,18},{10... | collective-permute-start | bytes 442376 | tf_op jit(solution)/shard_map/scores/ppermute | solution.py:335
  30.2 0.1 collective-permute-done.7
  30.3 0.6 %fusion = f32[8,224]{1,0:T(8,128)} fusion(f32[1,8,224]{2,1,0:T(8,128)S(1)} %collective-permute-done.7, f32[2,8,224]{2,1,0:T(8,128)S(1)} %slice_add_fusion.1), kind=kLoop, calls=%fused_computation.5 | loop fusion | flops 1792 | bytes 21504 | tf_op jit(solution)/shard_map/halve/squeeze | solution.py:407
  30.9 2.9 %collective-permute-done.3.refs_2_ = f32[9,16,256]{2,1,0:T(8,128)S(1)} collective-permute-done((f32[9,16,256]{2,1,0:T(8,128)S(1)}, f32[9,16,256]{2,1,0:T(8,128)S(1)}, u32[]{:S(2)}, u32[]{:S(2)}) %collective-permute-start.3) | collective-permute-done | bytes 147488 | tf_op jit(solution)/shard_map/scores/ppermute | solution.py:335
  33.8 0.9 %log_post.1 = f32[9,16,512]{2,1,0:T(8,128)} custom-call(f32[16,128]{1,0:T(8,128)S(1)} %get-tuple-element.28.total_ref, f32[9,16,128]{2,1,0:T(8,128)S(1)} %get-tuple-element.18.near_ref.refs_0_, f32[9,16,128]{2,1,0:T(8,128)S(1)} %get-tuple-element.29.refs_1_, f32[9,16,256]{2,1,0:T(8,128)S(1)} %collective-permute-done.3.refs_2_), custom_call_target="tpu_custom_call" | custom-call | flops 250000000 | bytes 500000 | tf_op jit(solution)/shard_map/order/log_post/pallas_call | solution.py:216
  (9 shorter events, 0.0 us)
Async XLA Ops:
  0.6 6.7 %collective-permute-start = (bf16[128,7168]{1,0:T(8,128)(2,1)}, bf16[128,7168]{1,0:T(8,128)(2,1)S(1)}, u32[]{:S(2)}, u32[]{:S(2)}) collective-permute-start(bf16[128,7168]{1,0:T(8,128)(2,1)} %refs_hbm.1), channel_id=1, source_target_pairs={{0,8},{8,0},{16,24},{24,16},{1,9},{9,1},{17,25},{25,17},{2,10},{10... | collective-permute-start | bytes 5505032 | tf_op jit(solution)/shard_map/references/ppermute | solution.py:335
  1.2 9.0 %collective-permute-start.1 = (bf16[16,7168]{1,0:T(8,128)(2,1)}, bf16[16,7168]{1,0:T(8,128)(2,1)S(1)}, u32[]{:S(2)}, u32[]{:S(2)}) collective-permute-start(bf16[16,7168]{1,0:T(8,128)(2,1)} %part_hbm.1), channel_id=1, source_target_pairs={{0,16},{8,24},{16,0},{24,8},{1,17},{9,25},{17,1},{25,9},{2,18},{10... | collective-permute-start | bytes 688136 | tf_op jit(solution)/shard_map/particles/ppermute | solution.py:335
  11.9 3.8 %collective-permute-start.2 = (f32[32,128]{1,0:T(8,128)S(1)}, f32[32,128]{1,0:T(8,128)S(1)}, u32[]{:S(2)}, u32[]{:S(2)}) collective-permute-start(f32[32,128]{1,0:T(8,128)S(1)} %constant_dynamic-update-slice_fusion.refs_0_), channel_id=1, source_target_pairs={{0,16},{8,24},{16,0},{24,8},{1,17},{9,25},{17,1},{25,9},{2,18},{10... | collective-permute-start | bytes 49160 | tf_op jit(solution)/shard_map/stats/ppermute | solution.py:335
  16.5 1.3 %collective-permute-start.4 = (f32[8,8,224]{2,1,0:T(8,128)S(1)}, f32[8,8,224]{2,1,0:T(8,128)S(1)}, u32[]{:S(2)}, u32[]{:S(2)}) collective-permute-start(f32[8,8,224]{2,1,0:T(8,128)S(1)} %slice_bitcast_fusion), channel_id=1, source_target_pairs={{0,8},{8,0},{16,24},{24,16},{1,9},{9,1},{17,25},{25,17},{2,10},{10... | collective-permute-start | bytes 172040 | tf_op jit(solution)/shard_map/halve/ppermute | solution.py:335
  17.8 4.9 %collective-permute-start.5 = (f32[4,8,224]{2,1,0:T(8,128)S(1)}, f32[4,8,224]{2,1,0:T(8,128)S(1)}, u32[]{:S(2)}, u32[]{:S(2)}) collective-permute-start(f32[4,8,224]{2,1,0:T(8,128)S(1)} %slice.33), channel_id=1, source_target_pairs={{0,4},{1,5},{2,6},{3,7},{4,0},{5,1},{6,2},{7,3},{8,12},{9,13},{10,... | collective-permute-start | bytes 86024 | tf_op jit(solution)/shard_map/halve/ppermute | solution.py:335
  22.7 3.8 %collective-permute-start.6 = (f32[2,8,224]{2,1,0:T(8,128)S(1)}, f32[2,8,224]{2,1,0:T(8,128)S(1)}, u32[]{:S(2)}, u32[]{:S(2)}) collective-permute-start(f32[2,8,224]{2,1,0:T(8,128)S(1)} %slice.35), channel_id=1, source_target_pairs={{0,2},{1,3},{2,0},{3,1},{4,6},{5,7},{6,4},{7,5},{8,10},{9,11},{10,... | collective-permute-start | bytes 43016 | tf_op jit(solution)/shard_map/halve/ppermute | solution.py:335
  26.5 3.7 %collective-permute-start.7 = (f32[1,8,224]{2,1,0:T(8,128)S(1)}, f32[1,8,224]{2,1,0:T(8,128)S(1)}, u32[]{:S(2)}, u32[]{:S(2)}) collective-permute-start(f32[1,8,224]{2,1,0:T(8,128)S(1)} %slice.37), channel_id=1, source_target_pairs={{0,1},{1,0},{2,3},{3,2},{4,5},{5,4},{6,7},{7,6},{8,9},{9,8},{10,11... | collective-permute-start | bytes 21512 | tf_op jit(solution)/shard_map/halve/ppermute | solution.py:335
  28.7 5.1 %collective-permute-start.3 = (f32[9,16,256]{2,1,0:T(8,128)S(1)}, f32[9,16,256]{2,1,0:T(8,128)S(1)}, u32[]{:S(2)}, u32[]{:S(2)}) collective-permute-start(f32[9,16,256]{2,1,0:T(8,128)S(1)} %get-tuple-element.30), channel_id=1, source_target_pairs={{0,16},{8,24},{16,0},{24,8},{1,17},{9,25},{17,1},{25,9},{2,18},{10... | collective-permute-start | bytes 442376 | tf_op jit(solution)/shard_map/scores/ppermute | solution.py:335

commit v3 on v2

--- a/solution.py
+++ b/solution.py
@@ -8,6 +8,7 @@
 from jax.experimental import pallas as pl
 from jax.experimental.pallas import tpu as pltpu
 from jax.sharding import PartitionSpec as P
+
 
 SHIFTS = 9
 PAIRS = 4
@@ -27,6 +28,14 @@
         right[:, None] * column_freq[None, :] + down[:, None] * row_freq[None, :]
     )
     return np.concatenate([np.cos(turning), np.sin(turning)], axis=0).astype(np.float32)
+
+
+def odd_bits(value):
+    return bin(value).count("1") % 2
+
+
+def mask_of(group):
+    return 2 * group + odd_bits(group)
 
 
 def chunks(total):
@@ -129,7 +138,7 @@
     return stats
 
 
-def near_body(classes, refs_hbm, part_hbm, table_hbm, weight_hbm, class_hbm, orient_hbm,
+def near_body(refs_hbm, part_hbm, table_hbm, weight_hbm, class_hbm, orient_hbm,
               class_prior_hbm, orient_prior_hbm, offset_hbm, scores_ref, bias_ref, tag_ref,
               refs_ref, part_ref, table_ref, weight_ref, class_ref,
               orient_ref, class_prior_ref, orient_prior_ref, offset_ref, small_sems, refs_sems):
@@ -212,7 +221,7 @@
 HBM = pl.BlockSpec(memory_space=pltpu.HBM)
 
 
-def call(body, name, shapes, specs, cost, *operands, scratch=()):
+def call(body, shapes, specs, cost, *operands, scratch=()):
     return pl.pallas_call(
         body,
         out_shape=[
@@ -223,7 +232,6 @@
         scratch_shapes=scratch,
         in_specs=specs,
         out_specs=[VMEM] * len(shapes),
-        name=name,
         compiler_params=pltpu.CompilerParams(vmem_limit_bytes=VMEM_LIMIT),
         cost_estimate=pl.CostEstimate(
             flops=int(cost * 5e8), bytes_accessed=int(cost * 1e6), transcendentals=0
@@ -301,21 +309,24 @@
     result = jnp.concatenate(pieces, axis=1)
     slots = sums_ref.shape[1]
     columns = sums_ref.shape[3]
+    side, rest = core, dom
+    for _ in range(slots.bit_length() - 1):
+        side, rest = lax.bitwise_xor(side, lax.rem(rest, 2)), rest // 2
     for half in range(2):
         for d in range(slots):
             at = (half * slots + d) * columns
-            sums_ref[lax.bitwise_xor(core, half), lax.bitwise_xor(dom, d)] = result[
+            sums_ref[lax.bitwise_xor(side, half ^ odd_bits(d)), lax.bitwise_xor(dom, d)] = result[
                 :, at : at + columns
             ]
 
 
-def order_body(block, groups, total_ref, *refs):
+def order_body(block, groups, masks, total_ref, *refs):
     out_ref = refs[-1]
     me = lax.axis_index("ref")
     slot = 0
     for ref in refs[:-1]:
         for at in range(0, ref.shape[2], block):
-            place = pl.multiple_of(lax.bitwise_xor(me, slot) * block, LANES)
+            place = pl.multiple_of(lax.bitwise_xor(me, masks[slot]) * block, LANES)
             for t in range(SHIFTS):
                 lift = total_ref[:, t * groups : t * groups + 1]
                 out_ref[t, :, pl.ds(place, block)] = ref[t, :, at : at + block] + lift
@@ -331,13 +342,16 @@
     groups = refs_axis // 2
     me = lax.axis_index("ref")
 
-    def swap(value, axis, size, bit):
-        return lax.ppermute(value, axis, [(i, i ^ bit) for i in range(size)])
-
-    with jax.named_scope("particles"):
-        others = [swap(particles, "ref", refs_axis, 2 * i) for i in range(1, groups)]
-    with jax.named_scope("references"):
-        peer_refs = swap(references, "ref", refs_axis, 1)
+    def swap(value, ref_mask, dom_mask):
+        pairs = [
+            (r * dom_axis + d, (r ^ ref_mask) * dom_axis + (d ^ dom_mask))
+            for r in range(refs_axis)
+            for d in range(dom_axis)
+        ]
+        return lax.ppermute(value, ("ref", "dom"), pairs)
+
+    others = [swap(particles, mask_of(i), 0) for i in range(1, groups)]
+    peer_refs = swap(references, 1, 0)
 
     table = jnp.asarray(turning_table(coefs))
     weight = noise_weight.reshape(coefs // LANES, LANES)
@@ -345,8 +359,7 @@
     orients = ref_orient.reshape(refs_axis, block)
     loaded = [references, particles, table, weight, kinds]
     near, prior, tag, *held = call(
-        functools.partial(near_body, classes),
-        "score_near",
+        near_body,
         [(SHIFTS, rows, block), (2, block), (rows, LANES)]
         + [jax.ShapeDtypeStruct(value.shape, value.dtype) for value in loaded],
         [HBM] * 9,
@@ -365,7 +378,6 @@
     shared = (table, weight, kinds)
     pair, bias, own_stats = call(
         functools.partial(pair_body, classes),
-        "score_pair",
         [(SHIFTS, rows, block), (2, block), (rows, LANES)],
         [VMEM] * 8,
         1.0,
@@ -375,7 +387,6 @@
     for other in others:
         value, stat = call(
             functools.partial(far_body, classes),
-            "score_far",
             [(SHIFTS, rows, 2 * block), (rows, LANES)],
             [VMEM] * 7,
             1.0,
@@ -384,43 +395,38 @@
         sent_scores.append(value)
         stats.append(stat)
     stats = jnp.concatenate(stats, axis=0)
-    with jax.named_scope("stats"):
-        seen = [stats] + [swap(stats, "ref", refs_axis, 2 * i) for i in range(1, groups)]
-    with jax.named_scope("scores"):
-        got = [swap(value, "ref", refs_axis, 2 * (i + 1)) for i, value in enumerate(sent_scores)]
+    seen = [stats] + [swap(stats, mask_of(i), 0) for i in range(1, groups)]
+    got = [swap(value, mask_of(i + 1), 0) for i, value in enumerate(sent_scores)]
     devices = refs_axis * dom_axis
-    with jax.named_scope("partial"):
-        sums, total = call(
-            functools.partial(sums_body, groups, classes, 1.0 / math.sqrt(rows * devices)),
-            "class_partial",
-            [(2, dom_axis, classes, width // devices), (rows, LANES)],
-            [VMEM] * (1 + 2 * groups),
-            1.0,
-            table, *seen, held_part, *others,
-        )
-    with jax.named_scope("halve"):
-        keep = sums[0] + swap(sums[1], "ref", refs_axis, 1)
-        slots = dom_axis
-        while slots > 1:
-            slots //= 2
-            keep = keep[:slots] + swap(keep[slots:], "dom", dom_axis, slots)
-        class_sums = keep[0]
+    sums, total = call(
+        functools.partial(sums_body, groups, classes, 1.0 / math.sqrt(rows * devices)),
+        [(2, dom_axis, classes, width // devices), (rows, LANES)],
+        [VMEM] * (1 + 2 * groups),
+        1.0,
+        table, *seen, held_part, *others,
+    )
+    keep = sums[0] + swap(sums[1], 1, 0)
+    slots = dom_axis
+    while slots > 1:
+        slots //= 2
+        keep = keep[:slots] + swap(keep[slots:], 1, slots)
+    class_sums = keep[0]
 
     blocks = [near, pair] + got
+    masks = [mask_of(i) ^ j for i in range(groups) for j in range(2)]
     if block % LANES == 0:
-        with jax.named_scope("order"):
-            (log_post,) = call(
-                functools.partial(order_body, block, classes),
-                "log_post",
-                [(SHIFTS, rows, refs_axis * block)],
-                [VMEM] * (1 + len(blocks)),
-                0.5,
-                total, *blocks,
-            )
+        (log_post,) = call(
+            functools.partial(order_body, block, classes, masks),
+            [(SHIFTS, rows, refs_axis * block)],
+            [VMEM] * (1 + len(blocks)),
+            0.5,
+            total, *blocks,
+        )
     else:
         pieces = [near, pair]
         for value in got:
             pieces += [value[:, :, :block], value[:, :, block:]]
+        pieces = [pieces[masks.index(j)] for j in range(refs_axis)]
         bit = 1
         while bit < refs_axis:
             pieces = [
@@ -433,8 +439,11 @@
 
 
 def solution(mesh):
+    def body(*args):
+        return local(mesh.shape["ref"], mesh.shape["dom"], *args)
+
     return jax.shard_map(
-        functools.partial(local, mesh.shape["ref"], mesh.shape["dom"]),
+        body,
         mesh=mesh,
         in_specs=(
             P(("ref", "dom"), None),

time: 34.9 us -> 32.8 us (0.940)
  starting transfers between devices: 13.4 us -> 11.5 us
    ppermute x8, starting transfers between devices: 13.4 us -> 11.5 us  [swap(): return lax.ppermute(value, ('ref', 'dom'), pairs)]
  transfers between devices with their start and end apart: 8 -> 8, of which waited for: 7 -> 7; matrix products, arithmetic and copies ran while one was open for 2% -> 2% of each run, Pallas kernels for 14% -> 15%
where the time goes in v3:
time: 32.8 us; the launch traced here: 32.7 us
  starting transfers between devices  11.5 us (35%)
  waiting for transfers between devices  11.4 us (35%)
  Pallas kernels  8.4 us (26%)
  between operations  0.71 us (2%)
  other arithmetic  0.62 us (2%)
    ppermute x8, starting transfers between devices, swap(): return lax.ppermute(value, ('ref', 'dom'), pairs)  11.5 us
    ppermute x8, waiting for transfers between devices, swap(): return lax.ppermute(value, ('ref', 'dom'), pairs)  11.4 us
    pallas_call x5, Pallas kernels, call(): pl.pallas_call(body, out_shape=[shape if isinstance(shape, jax.ShapeDtype...  8.4 us
  transfers between devices with their start and end apart: 8, of which 7 were waited for; matrix products, arithmetic and copies ran while one was open for 2% of the time, Pallas kernels for 15%

profile of v3, /device:TPU:0, one launch (start us, length us, event | category | flops | bytes accessed | tf_op | source)
XLA Modules:
  0.0 32.7 jit_solution(8244472013088022077)
XLA Ops:
  0.6 0.6 %collective-permute-start = (bf16[128,7168]{1,0:T(8,128)(2,1)}, bf16[128,7168]{1,0:T(8,128)(2,1)S(1)}, u32[]{:S(2)}, u32[]{:S(2)}) collective-permute-start(bf16[128,7168]{1,0:T(8,128)(2,1)} %refs_hbm.1), channel_id=1, source_target_pairs={{0,8},{1,9},{2,10},{3,11},{4,12},{5,13},{6,14},{7,15},{8,0},{9,1},... | collective-permute-start | bytes 5505032 | tf_op jit(solution)/shard_map/ppermute | solution.py:351
  1.2 2.6 %collective-permute-start.1 = (bf16[16,7168]{1,0:T(8,128)(2,1)}, bf16[16,7168]{1,0:T(8,128)(2,1)S(1)}, u32[]{:S(2)}, u32[]{:S(2)}) collective-permute-start(bf16[16,7168]{1,0:T(8,128)(2,1)} %part_hbm.1), channel_id=1, source_target_pairs={{0,24},{1,25},{2,26},{3,27},{4,28},{5,29},{6,30},{7,31},{8,16},{9,... | collective-permute-start | bytes 688136 | tf_op jit(solution)/shard_map/ppermute | solution.py:351
  3.8 3.5 %shard_map.104 = (f32[9,16,128]{2,1,0:T(8,128)S(1)}, f32[2,128]{1,0:T(2,128)S(1)}, f32[16,128]{1,0:T(8,128)S(1)}, bf16[128,7168]{1,0:T(8,128)(2,1)S(1)}, bf16[16...) custom-call(bf16[128,7168]{1,0:T(8,128)(2,1)} %refs_hbm.1, ...), custom_call_target="tpu_custom_call" | custom-call | flops 500000000 | bytes 1000000 | tf_op jit(solution)/shard_map/pallas_call | solution.py:225
  7.3 0.0 collective-permute-done.peer_ref
  7.3 1.5 %shard_map.105 = (f32[9,16,128]{2,1,0:T(8,128)S(1)}, f32[2,128]{1,0:T(2,128)S(1)}, f32[16,128]{1,0:T(8,128)S(1)}) custom-call(f32[9,16,128]{2,1,0:T(8,128)S(1)} %get-tuple-element.18.near_ref.refs_0_, bf16[128,7168]{1,0:T(8,128)(2,1)S(1)} %collective-permute-done.peer_ref, bf16[16,7168]{1,0:T(8,128)(2,1)S(1)} %get-tuple-element.19.part_ref.refs_2_, ...), custom_call_target="tpu_custom_call" | custom-call | flops 500000000 | bytes 1000000 | tf_op jit(solution)/shard_map/pallas_call | solution.py:225
  8.8 1.1 %collective-permute-done.1.part_ref.refs_3_ = bf16[16,7168]{1,0:T(8,128)(2,1)S(1)} collective-permute-done((bf16[16,7168]{1,0:T(8,128)(2,1)}, bf16[16,7168]{1,0:T(8,128)(2,1)S(1)}, u32[]{:S(2)}, u32[]{:S(2)}) %collective-permute-start.1) | collective-permute-done | bytes 229408 | tf_op jit(solution)/shard_map/ppermute | solution.py:351
  9.9 1.8 %shard_map.106 = (f32[9,16,256]{2,1,0:T(8,128)S(1)}, f32[16,128]{1,0:T(8,128)S(1)}) custom-call(bf16[128,7168]{1,0:T(8,128)(2,1)S(1)} %get-tuple-element.25.own_ref, bf16[128,7168]{1,0:T(8,128)(2,1)S(1)} %collective-permute-done.peer_ref, bf16[16,7168]{1,0:T(8,128)(2,1)S(1)} %collective-permute-done.1.part_ref.refs_3_, ...), custom_call_target="tpu_custom_call" | custom-call | flops 500000000 | bytes 1000000 | tf_op jit(solution)/shard_map/pallas_call | solution.py:225
  11.7 1.5 %collective-permute-start.2 = (f32[32,128]{1,0:T(8,128)S(1)}, f32[32,128]{1,0:T(8,128)S(1)}, u32[]{:S(2)}, u32[]{:S(2)}) collective-permute-start(f32[32,128]{1,0:T(8,128)S(1)} %constant_dynamic-update-slice_fusion.refs_0_), channel_id=1, source_target_pairs={{0,24},{1,25},{2,26},{3,27},{4,28},{5,29},{6,30},{7,31},{8,16},{9,... | collective-permute-start | bytes 49160 | tf_op jit(solution)/shard_map/ppermute | solution.py:351
  13.1 1.8 %collective-permute-done.2.refs_1_ = f32[32,128]{1,0:T(8,128)S(1)} collective-permute-done((f32[32,128]{1,0:T(8,128)S(1)}, f32[32,128]{1,0:T(8,128)S(1)}, u32[]{:S(2)}, u32[]{:S(2)}) %collective-permute-start.2) | collective-permute-done | bytes 16416 | tf_op jit(solution)/shard_map/ppermute | solution.py:351
  14.9 0.7 %shard_map.107 = (f32[2,8,8,224]{3,2,1,0:T(8,128)S(1)}, f32[16,128]{1,0:T(8,128)S(1)}) custom-call(f32[8,3584]{1,0:T(8,128)S(1)} %get-tuple-element.17.table_ref, f32[32,128]{1,0:T(8,128)S(1)} %constant_dynamic-update-slice_fusion.refs_0_, f32[32,128]{1,0:T(8,128)S(1)} %collective-permute-done.2.refs_1_, ...), custom_call_target="tpu_custom_call" | custom-call | flops 500000000 | bytes 1000000 | tf_op jit(solution)/shard_map/pallas_call | solution.py:225
  15.7 0.2 collective-permute-start.4
  15.8 1.1 %collective-permute-done.4 = f32[8,8,224]{2,1,0:T(8,128)S(1)} collective-permute-done((f32[8,8,224]{2,1,0:T(8,128)S(1)}, f32[8,8,224]{2,1,0:T(8,128)S(1)}, u32[]{:S(2)}, u32[]{:S(2)}) %collective-permute-start.4) | collective-permute-done | bytes 57376 | tf_op jit(solution)/shard_map/ppermute | solution.py:351
  17.0 2.6 %collective-permute-start.5 = (f32[4,8,224]{2,1,0:T(8,128)S(1)}, f32[4,8,224]{2,1,0:T(8,128)S(1)}, u32[]{:S(2)}, u32[]{:S(2)}) collective-permute-start(f32[4,8,224]{2,1,0:T(8,128)S(1)} %slice.33), channel_id=1, source_target_pairs={{0,12},{1,13},{2,14},{3,15},{4,8},{5,9},{6,10},{7,11},{8,4},{9,5},... | collective-permute-start | bytes 86024 | tf_op jit(solution)/shard_map/ppermute | solution.py:351
  19.6 1.8 %collective-permute-done.5 = f32[4,8,224]{2,1,0:T(8,128)S(1)} collective-permute-done((f32[4,8,224]{2,1,0:T(8,128)S(1)}, f32[4,8,224]{2,1,0:T(8,128)S(1)}, u32[]{:S(2)}, u32[]{:S(2)}) %collective-permute-start.5) | collective-permute-done | bytes 28704 | tf_op jit(solution)/shard_map/ppermute | solution.py:351
  21.3 1.5 %collective-permute-start.6 = (f32[2,8,224]{2,1,0:T(8,128)S(1)}, f32[2,8,224]{2,1,0:T(8,128)S(1)}, u32[]{:S(2)}, u32[]{:S(2)}) collective-permute-start(f32[2,8,224]{2,1,0:T(8,128)S(1)} %slice.35), channel_id=1, source_target_pairs={{0,10},{1,11},{2,8},{3,9},{4,14},{5,15},{6,12},{7,13},{8,2},{9,3},... | collective-permute-start | bytes 43016 | tf_op jit(solution)/shard_map/ppermute | solution.py:351
  22.9 1.7 %collective-permute-done.6 = f32[2,8,224]{2,1,0:T(8,128)S(1)} collective-permute-done((f32[2,8,224]{2,1,0:T(8,128)S(1)}, f32[2,8,224]{2,1,0:T(8,128)S(1)}, u32[]{:S(2)}, u32[]{:S(2)}) %collective-permute-start.6) | collective-permute-done | bytes 14368 | tf_op jit(solution)/shard_map/ppermute | solution.py:351
  24.6 1.4 %collective-permute-start.7 = (f32[1,8,224]{2,1,0:T(8,128)S(1)}, f32[1,8,224]{2,1,0:T(8,128)S(1)}, u32[]{:S(2)}, u32[]{:S(2)}) collective-permute-start(f32[1,8,224]{2,1,0:T(8,128)S(1)} %slice.37), channel_id=1, source_target_pairs={{0,9},{1,8},{2,11},{3,10},{4,13},{5,12},{6,15},{7,14},{8,1},{9,0},... | collective-permute-start | bytes 21512 | tf_op jit(solution)/shard_map/ppermute | solution.py:351
  26.0 1.2 %collective-permute-start.3 = (f32[9,16,256]{2,1,0:T(8,128)S(1)}, f32[9,16,256]{2,1,0:T(8,128)S(1)}, u32[]{:S(2)}, u32[]{:S(2)}) collective-permute-start(f32[9,16,256]{2,1,0:T(8,128)S(1)} %get-tuple-element.30), channel_id=1, source_target_pairs={{0,24},{1,25},{2,26},{3,27},{4,28},{5,29},{6,30},{7,31},{8,16},{9,... | collective-permute-start | bytes 442376 | tf_op jit(solution)/shard_map/ppermute | solution.py:351
  27.2 0.4 %collective-permute-done.7 = f32[1,8,224]{2,1,0:T(8,128)S(1)} collective-permute-done((f32[1,8,224]{2,1,0:T(8,128)S(1)}, f32[1,8,224]{2,1,0:T(8,128)S(1)}, u32[]{:S(2)}, u32[]{:S(2)}) %collective-permute-start.7) | collective-permute-done | bytes 7200 | tf_op jit(solution)/shard_map/ppermute | solution.py:351
  27.6 0.6 %fusion = f32[8,224]{1,0:T(8,128)} fusion(f32[1,8,224]{2,1,0:T(8,128)S(1)} %collective-permute-done.7, f32[2,8,224]{2,1,0:T(8,128)S(1)} %slice_add_fusion.1), kind=kLoop, calls=%fused_computation.5 | loop fusion | flops 1792 | bytes 21504 | tf_op jit(solution)/shard_map/squeeze | solution.py:413
  28.2 3.5 %collective-permute-done.3.refs_2_ = f32[9,16,256]{2,1,0:T(8,128)S(1)} collective-permute-done((f32[9,16,256]{2,1,0:T(8,128)S(1)}, f32[9,16,256]{2,1,0:T(8,128)S(1)}, u32[]{:S(2)}, u32[]{:S(2)}) %collective-permute-start.3) | collective-permute-done | bytes 147488 | tf_op jit(solution)/shard_map/ppermute | solution.py:351
  31.8 0.9 %shard_map.108 = f32[9,16,512]{2,1,0:T(8,128)} custom-call(f32[16,128]{1,0:T(8,128)S(1)} %get-tuple-element.28.total_ref, f32[9,16,128]{2,1,0:T(8,128)S(1)} %get-tuple-element.18.near_ref.refs_0_, f32[9,16,128]{2,1,0:T(8,128)S(1)} %get-tuple-element.29.refs_1_, f32[9,16,256]{2,1,0:T(8,128)S(1)} %collective-permute-done.3.refs_2_), custom_call_target="tpu_custom_call" | custom-call | flops 250000000 | bytes 500000 | tf_op jit(solution)/shard_map/pallas_call | solution.py:225
  (9 shorter events, 0.0 us)
Async XLA Ops:
  0.6 6.7 %collective-permute-start = (bf16[128,7168]{1,0:T(8,128)(2,1)}, bf16[128,7168]{1,0:T(8,128)(2,1)S(1)}, u32[]{:S(2)}, u32[]{:S(2)}) collective-permute-start(bf16[128,7168]{1,0:T(8,128)(2,1)} %refs_hbm.1), channel_id=1, source_target_pairs={{0,8},{1,9},{2,10},{3,11},{4,12},{5,13},{6,14},{7,15},{8,0},{9,1},... | collective-permute-start | bytes 5505032 | tf_op jit(solution)/shard_map/ppermute | solution.py:351
  1.2 8.7 %collective-permute-start.1 = (bf16[16,7168]{1,0:T(8,128)(2,1)}, bf16[16,7168]{1,0:T(8,128)(2,1)S(1)}, u32[]{:S(2)}, u32[]{:S(2)}) collective-permute-start(bf16[16,7168]{1,0:T(8,128)(2,1)} %part_hbm.1), channel_id=1, source_target_pairs={{0,24},{1,25},{2,26},{3,27},{4,28},{5,29},{6,30},{7,31},{8,16},{9,... | collective-permute-start | bytes 688136 | tf_op jit(solution)/shard_map/ppermute | solution.py:351
  11.7 3.2 %collective-permute-start.2 = (f32[32,128]{1,0:T(8,128)S(1)}, f32[32,128]{1,0:T(8,128)S(1)}, u32[]{:S(2)}, u32[]{:S(2)}) collective-permute-start(f32[32,128]{1,0:T(8,128)S(1)} %constant_dynamic-update-slice_fusion.refs_0_), channel_id=1, source_target_pairs={{0,24},{1,25},{2,26},{3,27},{4,28},{5,29},{6,30},{7,31},{8,16},{9,... | collective-permute-start | bytes 49160 | tf_op jit(solution)/shard_map/ppermute | solution.py:351
  15.7 1.3 %collective-permute-start.4 = (f32[8,8,224]{2,1,0:T(8,128)S(1)}, f32[8,8,224]{2,1,0:T(8,128)S(1)}, u32[]{:S(2)}, u32[]{:S(2)}) collective-permute-start(f32[8,8,224]{2,1,0:T(8,128)S(1)} %slice_bitcast_fusion), channel_id=1, source_target_pairs={{0,8},{1,9},{2,10},{3,11},{4,12},{5,13},{6,14},{7,15},{8,0},{9,1},... | collective-permute-start | bytes 172040 | tf_op jit(solution)/shard_map/ppermute | solution.py:351
  17.0 4.3 %collective-permute-start.5 = (f32[4,8,224]{2,1,0:T(8,128)S(1)}, f32[4,8,224]{2,1,0:T(8,128)S(1)}, u32[]{:S(2)}, u32[]{:S(2)}) collective-permute-start(f32[4,8,224]{2,1,0:T(8,128)S(1)} %slice.33), channel_id=1, source_target_pairs={{0,12},{1,13},{2,14},{3,15},{4,8},{5,9},{6,10},{7,11},{8,4},{9,5},... | collective-permute-start | bytes 86024 | tf_op jit(solution)/shard_map/ppermute | solution.py:351
  21.3 3.2 %collective-permute-start.6 = (f32[2,8,224]{2,1,0:T(8,128)S(1)}, f32[2,8,224]{2,1,0:T(8,128)S(1)}, u32[]{:S(2)}, u32[]{:S(2)}) collective-permute-start(f32[2,8,224]{2,1,0:T(8,128)S(1)} %slice.35), channel_id=1, source_target_pairs={{0,10},{1,11},{2,8},{3,9},{4,14},{5,15},{6,12},{7,13},{8,2},{9,3},... | collective-permute-start | bytes 43016 | tf_op jit(solution)/shard_map/ppermute | solution.py:351
  24.6 3.1 %collective-permute-start.7 = (f32[1,8,224]{2,1,0:T(8,128)S(1)}, f32[1,8,224]{2,1,0:T(8,128)S(1)}, u32[]{:S(2)}, u32[]{:S(2)}) collective-permute-start(f32[1,8,224]{2,1,0:T(8,128)S(1)} %slice.37), channel_id=1, source_target_pairs={{0,9},{1,8},{2,11},{3,10},{4,13},{5,12},{6,15},{7,14},{8,1},{9,0},... | collective-permute-start | bytes 21512 | tf_op jit(solution)/shard_map/ppermute | solution.py:351
  26.0 5.8 %collective-permute-start.3 = (f32[9,16,256]{2,1,0:T(8,128)S(1)}, f32[9,16,256]{2,1,0:T(8,128)S(1)}, u32[]{:S(2)}, u32[]{:S(2)}) collective-permute-start(f32[9,16,256]{2,1,0:T(8,128)S(1)} %get-tuple-element.30), channel_id=1, source_target_pairs={{0,24},{1,25},{2,26},{3,27},{4,28},{5,29},{6,30},{7,31},{8,16},{9,... | collective-permute-start | bytes 442376 | tf_op jit(solution)/shard_map/ppermute | solution.py:351
